TPU v7x, 32 devices: a whole 2x2x4 slice. The times are simulated.
32 devices in a mesh: dp: 8 (over y, x, core), tensor: 4 (over z).
Axes of the slice: x: 2, y: 2, z: 4, core: 2. Of those that a mesh axis runs over, the one named last changes fastest.
Arguments:
- tokens: bfloat16 [16384, 768], P(('dp', 'tensor')), may hold values from -6 to 6
- teacher: bfloat16 [16384, 768], P(('dp', 'tensor')), may hold values from -6 to 6
- lengths: int32 [8], P('dp'), may hold values from 256 to 2048, as said below
- loss_mask: int32 [16384], P(('dp', 'tensor')), may hold values 0 or 1
- loss_scale: float32 [], replicated, may hold values from 1572864 to 6291456
- query_weight: bfloat16 [768, 768], P('dp', 'tensor'), may hold values from -0.21875 to 0.21875
- query_bias: bfloat16 [768], P('dp'), may hold values from -3 to 3
- key_weight: bfloat16 [768, 768], P('dp', 'tensor'), may hold values from -0.21875 to 0.21875
- value_weight: bfloat16 [768, 768], P('dp', 'tensor'), may hold values from -0.21875 to 0.21875
- value_bias: bfloat16 [768], P('dp'), may hold values from -3 to 3
- mixer_weight: bfloat16 [768, 768], P('tensor', 'dp'), may hold values from -6 to 6
- mixer_bias: bfloat16 [768], P('dp'), may hold values from -3 to 3
- first_gain: bfloat16 [768], P('dp'), may hold values from 0.5 to 1.5
- first_shift: bfloat16 [768], P('dp'), may hold values from -3 to 3
- inner_weight: bfloat16 [768, 3072], P('dp', 'tensor'), may hold values from -0.21875 to 0.21875
- inner_bias: bfloat16 [3072], P('dp'), may hold values from -3 to 3
- outer_weight: bfloat16 [3072, 768], P('tensor', 'dp'), may hold values from -0.15625 to 0.15625
- outer_bias: bfloat16 [768], P('dp'), may hold values from -3 to 3
- second_gain: bfloat16 [768], P('dp'), may hold values from 0.5 to 1.5
- second_shift: bfloat16 [768], P('dp'), may hold values from -3 to 3
Outputs:
- layer_output: bfloat16 [16384, 768], P(('dp', 'tensor'))
- loss_value: float32 [], replicated
- input_grad: float32 [16384, 768], P(('dp', 'tensor'))
- query_grad: float32 [768, 768], P('dp', 'tensor')
- querybias_grad: float32 [768], P('dp')
- key_grad: float32 [768, 768], P('dp', 'tensor')
- value_grad: float32 [768, 768], P('dp', 'tensor')
- valuebias_grad: float32 [768], P('dp')
- mixer_grad: float32 [768, 768], P('tensor', 'dp')
- mixerbias_grad: float32 [768], P('dp')
- firstgain_grad: float32 [768], P('dp')
- firstshift_grad: float32 [768], P('dp')
- inner_grad: float32 [768, 3072], P('dp', 'tensor')
- innerbias_grad: float32 [3072], P('dp')
- outer_grad: float32 [3072, 768], P('tensor', 'dp')
- outerbias_grad: float32 [768], P('dp')
- secondgain_grad: float32 [768], P('dp')
- secondshift_grad: float32 [768], P('dp')
Inputs may be any that keep to these rules, and one draw needn't show every extreme that they name: lengths[s] is how many leading tokens of sequence s are valid; the rest are padding. Some sequence has exactly 2048 and another exactly one eighth of 2048.
All inputs are finite; a program needn't handle non-finite values. No bound on the sum of `loss_mask` on one device may be relied on, other than what follows from the above.
Results may differ from a plain program's by a relative error of at most 0.018.
Values may be sent and summed in bfloat16 or wider, within the bound.
A program may use at most 128 MiB of HBM per device.

v0:
```python
import jax
import jax.numpy as jnp
from jax import lax
from jax.sharding import PartitionSpec as P

HEAD_DIM = 64
QBLOCK = 512


norm_eps = 1e-05
masked_score = -1e30


def in_blocks(value, dim, size):
    before, after = (value.shape[:dim], value.shape[dim + 1 :])
    return jnp.moveaxis(value.reshape(*before, size, -1, *after), dim, 0)


def summed_on_arrival(value, axis, dim):
    size = lax.axis_size(axis)
    blocks = lax.all_to_all(in_blocks(value, dim, size), axis, 0, 0, tiled=True)
    return jnp.sum(blocks.astype(jnp.float32), axis=0)


def sent_together(arrays, axis, dim, along):
    both = jnp.concatenate(arrays, axis=along)
    out, at, gathered = (summed_on_arrival(both, axis, dim), 0, [])
    for a in arrays:
        gathered.append(lax.slice_in_dim(out, at, at + a.shape[along], axis=along))
        at += a.shape[along]
    return tuple(gathered)


def contract_last(left_rows, right_rows):
    return lax.dot_general(
        left_rows, right_rows, (((1,), (1,)), ((), ())), preferred_element_type=jnp.float32
    )


def contract_first(left_rows, right_rows):
    return lax.dot_general(
        left_rows, right_rows, (((0,), (0,)), ((), ())), preferred_element_type=jnp.float32
    )


def plain_dot(left_rows, right_rows):
    return jnp.dot(left_rows, right_rows, preferred_element_type=jnp.float32)


def gelu_exact(pre_values):
    return jax.nn.gelu(pre_values, approximate=False)


def norm_forward(values_in, gain_vec, shift_vec):
    centred = values_in - jnp.mean(values_in, axis=1, keepdims=True)
    inv_std = lax.rsqrt(jnp.mean(centred * centred, axis=1, keepdims=True) + norm_eps)
    normed = centred * inv_std
    return (normed * gain_vec + shift_vec, normed, inv_std)


def norm_backward(grad_out, normed, inv_std, gain_vec):
    grad_normed = grad_out * gain_vec
    mean_plain = jnp.mean(grad_normed, axis=1, keepdims=True)
    mean_mixed = jnp.mean(grad_normed * normed, axis=1, keepdims=True)
    grad_in = inv_std * (grad_normed - mean_plain - normed * mean_mixed)
    return (grad_in, jnp.sum(grad_out * normed, axis=0), jnp.sum(grad_out, axis=0))


def shards(
    tokens,
    teacher,
    lengths,
    loss_mask,
    loss_scale,
    query_weight,
    query_bias,
    key_weight,
    value_weight,
    value_bias,
    mixer_weight,
    mixer_bias,
    first_gain,
    first_shift,
    inner_weight,
    inner_bias,
    outer_weight,
    outer_bias,
    second_gain,
    second_shift,
):
    tp_count = lax.axis_size("tensor")
    tp_index = lax.axis_index("tensor")
    dp_count = lax.axis_size("dp")
    dp_index = lax.axis_index("dp")
    local_rows = tokens.shape[0]
    seq_len = local_rows * tp_count
    model_width = tokens.shape[1]
    head_width = query_weight.shape[1]
    hidden_width = inner_weight.shape[1]
    head_count = head_width // HEAD_DIM
    block_count = seq_len // QBLOCK
    score_scale = HEAD_DIM ** (-0.5)
    length_here = lengths[0]
    local_pos = tp_index * local_rows + jnp.arange(local_rows)
    counted = jnp.logical_and(local_pos < length_here, loss_mask == 1).astype(jnp.float32)
    count_local = jnp.sum(counted)
    small_stack = jnp.stack(
        [
            query_bias,
            value_bias,
            mixer_bias,
            first_gain,
            first_shift,
            outer_bias,
            second_gain,
            second_shift,
        ]
    )

    def fetch_params():
        return (
            lax.all_gather(query_weight, "dp", axis=0, tiled=True),
            lax.all_gather(key_weight, "dp", axis=0, tiled=True),
            lax.all_gather(value_weight, "dp", axis=0, tiled=True),
            lax.all_gather(mixer_weight, "dp", axis=1, tiled=True),
            lax.all_gather(inner_weight, "dp", axis=0, tiled=True),
            lax.all_gather(outer_weight, "dp", axis=1, tiled=True),
            lax.all_gather(small_stack, "dp", axis=1, tiled=True),
            lax.all_gather(inner_bias, "dp", axis=0, tiled=True),
        )

    def attn_gather(values_in):
        return lax.all_gather(values_in, "tensor", axis=0, tiled=True)

    def ffn_gather(values_in):
        return lax.all_gather(values_in, "tensor", axis=0, tiled=True)

    (
        query_full,
        key_full,
        value_full,
        mixer_full,
        inner_full,
        outer_full,
        small_full,
        innerb_full,
    ) = fetch_params()
    small_wide = small_full.astype(jnp.float32)
    qbias_mine = lax.dynamic_slice_in_dim(small_wide[0], tp_index * head_width, head_width)
    vbias_mine = lax.dynamic_slice_in_dim(small_wide[1], tp_index * head_width, head_width)
    inner_mine = lax.dynamic_slice_in_dim(
        innerb_full.astype(jnp.float32), tp_index * hidden_width, hidden_width
    )
    seq_rows = attn_gather(tokens)
    queries = (plain_dot(seq_rows, query_full) + qbias_mine).astype(jnp.bfloat16)
    keys_all = plain_dot(seq_rows, key_full).astype(jnp.bfloat16)
    values_all = (plain_dot(seq_rows, value_full) + vbias_mine).astype(jnp.bfloat16)
    keys_three = keys_all.reshape(seq_len, head_count, HEAD_DIM)
    values_three = values_all.reshape(seq_len, head_count, HEAD_DIM)
    key_valid = jnp.arange(seq_len) < length_here

    def score_block(query_block):
        scores = (
            jnp.einsum("qhd,khd->hqk", query_block, keys_three, preferred_element_type=jnp.float32)
            * score_scale
        )
        return jnp.where(key_valid[None, None, :], scores, masked_score)

    def forward_block(query_block):
        scores = score_block(query_block)
        row_top = jnp.max(scores, axis=2, keepdims=True)
        exp_scores = jnp.exp(scores - row_top)
        row_total = jnp.sum(exp_scores, axis=2, keepdims=True)
        prob_low = (exp_scores / row_total).astype(jnp.bfloat16)
        mixed_rows = jnp.einsum(
            "hqk,khd->qhd", prob_low, values_three, preferred_element_type=jnp.float32
        )
        return (mixed_rows.astype(jnp.bfloat16), (row_top + jnp.log(row_total))[:, :, 0])

    query_blocks = queries.reshape(block_count, QBLOCK, head_count, HEAD_DIM)
    attended, log_sums = lax.map(forward_block, query_blocks)
    attended = attended.reshape(seq_len, head_width)
    attn_out = lax.psum_scatter(
        plain_dot(attended, mixer_full).astype(jnp.bfloat16),
        "tensor",
        scatter_dimension=0,
        tiled=True,
    ).astype(jnp.float32)
    first_sum = tokens.astype(jnp.float32) + attn_out + small_wide[2]
    hidden_one, normed_one, inv_one = norm_forward(first_sum, small_wide[3], small_wide[4])
    hidden_low = hidden_one.astype(jnp.bfloat16)
    ffn_rows = ffn_gather(hidden_low)
    pre_act = plain_dot(ffn_rows, inner_full) + inner_mine
    act_full, gelu_pull = jax.vjp(gelu_exact, pre_act)
    activated = act_full.astype(jnp.bfloat16)
    ffn_out = lax.psum_scatter(
        plain_dot(activated, outer_full).astype(jnp.bfloat16),
        "tensor",
        scatter_dimension=0,
        tiled=True,
    ).astype(jnp.float32)
    second_sum = hidden_one + ffn_out + small_wide[5]
    final_rows, normed_two, inv_two = norm_forward(second_sum, small_wide[6], small_wide[7])
    layer_output = final_rows.astype(jnp.bfloat16)
    diff_rows = final_rows - teacher.astype(jnp.float32)
    loss_local = jnp.sum(counted * jnp.sum(diff_rows * diff_rows, axis=1))
    loss_total, token_total = lax.psum((loss_local, count_local), ("dp", "tensor"))
    grad_scale = 2.0 * loss_scale / (token_total * model_width)
    grad_final = grad_scale * counted[:, None] * diff_rows
    (
        query_full,
        key_full,
        value_full,
        mixer_full,
        inner_full,
        outer_full,
        small_full,
        innerb_full,
    ) = fetch_params()
    ffn_rows = ffn_gather(hidden_low)
    grad_second, secondgain_part, secondshift_part = norm_backward(
        grad_final, normed_two, inv_two, small_wide[6]
    )
    outerbias_part = jnp.sum(grad_second, axis=0)
    grad_ffn_rows = lax.all_gather(grad_second.astype(jnp.bfloat16), "tensor", axis=0, tiled=True)
    grad_act = contract_last(grad_ffn_rows, outer_full)
    outer_local = contract_first(activated, grad_ffn_rows)
    grad_pre = gelu_pull(grad_act)[0].astype(jnp.bfloat16)
    innerbias_part = jnp.sum(grad_pre, axis=0, dtype=jnp.float32)
    inner_local = contract_first(ffn_rows, grad_pre)
    grad_hidden = lax.psum_scatter(
        contract_last(grad_pre, inner_full).astype(jnp.bfloat16),
        "tensor",
        scatter_dimension=0,
        tiled=True,
    ).astype(jnp.float32)
    inner_grad, outer_grad = (
        lax.psum_scatter(inner_local, "dp", scatter_dimension=0, tiled=True),
        lax.psum_scatter(outer_local, "dp", scatter_dimension=1, tiled=True),
    )
    grad_first, firstgain_part, firstshift_part = norm_backward(
        grad_second + grad_hidden, normed_one, inv_one, small_wide[3]
    )
    mixerbias_part = jnp.sum(grad_first, axis=0)
    grad_attn_rows = lax.all_gather(grad_first.astype(jnp.bfloat16), "tensor", axis=0, tiled=True)
    grad_attended = contract_last(grad_attn_rows, mixer_full).astype(jnp.bfloat16)
    mixer_local = contract_first(attended, grad_attn_rows)
    grad_blocks = grad_attended.reshape(block_count, QBLOCK, head_count, HEAD_DIM)

    def backward_block(carried, block_in):
        key_acc, value_acc = carried
        query_block, grad_block, lse_block = block_in
        scores = score_block(query_block)
        prob_full = jnp.exp(scores - lse_block[:, :, None])
        prob_low = prob_full.astype(jnp.bfloat16)
        grad_prob = jnp.einsum(
            "qhd,khd->hqk", grad_block, values_three, preferred_element_type=jnp.float32
        )
        row_dot = jnp.sum(prob_full * grad_prob, axis=2, keepdims=True)
        grad_scores = (prob_full * (grad_prob - row_dot)).astype(jnp.bfloat16)
        grad_query = (
            jnp.einsum("hqk,khd->qhd", grad_scores, keys_three, preferred_element_type=jnp.float32)
            * score_scale
        ).astype(jnp.bfloat16)
        key_acc = (
            key_acc
            + jnp.einsum(
                "hqk,qhd->khd", grad_scores, query_block, preferred_element_type=jnp.float32
            )
            * score_scale
        )
        value_acc = value_acc + jnp.einsum(
            "hqk,qhd->khd", prob_low, grad_block, preferred_element_type=jnp.float32
        )
        return ((key_acc, value_acc), grad_query)

    zero_acc = jnp.zeros((seq_len, head_count, HEAD_DIM), jnp.float32)
    (key_acc, value_acc), grad_queries = lax.scan(
        backward_block, (zero_acc, zero_acc), (query_blocks, grad_blocks, log_sums)
    )
    grad_queries = grad_queries.reshape(seq_len, head_width)
    grad_keys = key_acc.reshape(seq_len, head_width).astype(jnp.bfloat16)
    grad_values = value_acc.reshape(seq_len, head_width).astype(jnp.bfloat16)
    seq_rows = attn_gather(tokens)
    query_local = contract_first(seq_rows, grad_queries)
    key_local = contract_first(seq_rows, grad_keys)
    value_local = contract_first(seq_rows, grad_values)
    querybias_part = jnp.sum(grad_queries, axis=0, dtype=jnp.float32)
    valuebias_part = jnp.sum(grad_values, axis=0, dtype=jnp.float32)
    total_term = contract_last(grad_queries, query_full)
    total_term = total_term + contract_last(grad_keys, key_full)
    grad_tokens = lax.psum_scatter(
        (total_term + contract_last(grad_values, value_full)).astype(jnp.bfloat16),
        "tensor",
        scatter_dimension=0,
        tiled=True,
    ).astype(jnp.float32)
    input_grad = grad_first + grad_tokens
    query_grad, key_grad, value_grad, mixer_grad = (
        *sent_together(
            (
                query_local.astype(jnp.bfloat16),
                key_local.astype(jnp.bfloat16),
                value_local.astype(jnp.bfloat16),
            ),
            "dp",
            0,
            1,
        ),
        summed_on_arrival(mixer_local.astype(jnp.bfloat16), "dp", 1),
    )

    def spread_part(part_vec, full_width):
        return lax.dynamic_update_slice_in_dim(
            jnp.zeros((full_width,), jnp.float32), part_vec, tp_index * part_vec.shape[0], 0
        )

    small_terms = jnp.stack(
        [
            spread_part(querybias_part, model_width),
            spread_part(valuebias_part, model_width),
            mixerbias_part,
            firstgain_part,
            firstshift_part,
            outerbias_part,
            secondgain_part,
            secondshift_part,
        ]
    )
    inner_terms = spread_part(innerbias_part, hidden_width * tp_count)
    small_sum, inner_sum = lax.psum((small_terms, inner_terms), ("dp", "tensor"))
    loss_value = loss_total / (token_total * model_width)
    width_share = model_width // dp_count
    small_mine = lax.dynamic_slice_in_dim(small_sum, dp_index * width_share, width_share, 1)
    hidden_share = inner_sum.shape[0] // dp_count
    innerbias_grad = lax.dynamic_slice_in_dim(inner_sum, dp_index * hidden_share, hidden_share, 0)
    return (
        layer_output,
        loss_value,
        input_grad,
        query_grad,
        small_mine[0],
        key_grad,
        value_grad,
        small_mine[1],
        mixer_grad,
        small_mine[2],
        small_mine[3],
        small_mine[4],
        inner_grad,
        innerbias_grad,
        outer_grad,
        small_mine[5],
        small_mine[6],
        small_mine[7],
    )


def solution(mesh):
    return jax.shard_map(
        shards,
        mesh=mesh,
        in_specs=(
            P(("dp", "tensor"), None),
            P(("dp", "tensor"), None),
            P("dp"),
            P(("dp", "tensor")),
            P(),
            P("dp", "tensor"),
            P("dp"),
            P("dp", "tensor"),
            P("dp", "tensor"),
            P("dp"),
            P("tensor", "dp"),
            P("dp"),
            P("dp"),
            P("dp"),
            P("dp", "tensor"),
            P("dp"),
            P("tensor", "dp"),
            P("dp"),
            P("dp"),
            P("dp"),
        ),
        out_specs=(
            P(("dp", "tensor"), None),
            P(),
            P(("dp", "tensor"), None),
            P("dp", "tensor"),
            P("dp"),
            P("dp", "tensor"),
            P("dp", "tensor"),
            P("dp"),
            P("tensor", "dp"),
            P("dp"),
            P("dp"),
            P("dp"),
            P("dp", "tensor"),
            P("dp"),
            P("tensor", "dp"),
            P("dp"),
            P("dp"),
            P("dp"),
        ),
        check_vma=False,
    )
```

profile of v0, /device:TPU:0, one launch (start us, length us, event | category | flops | bytes accessed | tf_op | source)
XLA Modules:
  0.0 855.1 jit_solution(3259111184380616328)
XLA Ops:
  9.6 10.4 %all-gather = bf16[8,96,8]{1,2,0:T(8,128)(2,1)S(1)} all-gather(bf16[1,96,8]{1,2,0:T(8,128)(2,1)S(1)} %bitcast.198), channel_id=1, replica_groups=mesh['dp'=8,'tensor'=4] {'dp'}, dimensions={0}, use_global_device_ids=true | all-gather | bytes 13824 | tf_op jit(solution)/shard_map/all_gather | solution.py:128
  21.0 9.6 %all_gather.49 = bf16[192,768]{0,1:T(8,128)(2,1)S(1)} all-gather(bf16[192,96]{0,1:T(8,128)(2,1)S(1)} %copy.51), channel_id=1, replica_groups=mesh['dp'=8,'tensor'=4] {'dp'}, dimensions={1}, use_global_device_ids=true | all-gather | bytes 331776 | tf_op jit(solution)/shard_map/all_gather | solution.py:125
  30.6 8.8 %all_gather.45 = bf16[768,192]{1,0:T(8,128)(2,1)S(1)} all-gather(bf16[96,192]{1,0:T(8,128)(2,1)} %param.29), channel_id=1, replica_groups=mesh['dp'=8,'tensor'=4] {'dp'}, dimensions={0}, use_global_device_ids=true | all-gather | bytes 331776 | tf_op jit(solution)/shard_map/all_gather | solution.py:122
  39.4 9.3 %all_gather.47 = bf16[768,192]{1,0:T(8,128)(2,1)S(1)} all-gather(bf16[96,192]{1,0:T(8,128)(2,1)} %param.31), channel_id=1, replica_groups=mesh['dp'=8,'tensor'=4] {'dp'}, dimensions={0}, use_global_device_ids=true | all-gather | bytes 331776 | tf_op jit(solution)/shard_map/all_gather | solution.py:123
  48.7 9.0 %all_gather.48 = bf16[768,192]{1,0:T(8,128)(2,1)S(1)} all-gather(bf16[96,192]{1,0:T(8,128)(2,1)} %param.32), channel_id=1, replica_groups=mesh['dp'=8,'tensor'=4] {'dp'}, dimensions={0}, use_global_device_ids=true | all-gather | bytes 331776 | tf_op jit(solution)/shard_map/all_gather | solution.py:124
  58.6 18.0 %all-gather.9.cloned.1.call-done = bf16[2048,768]{1,0:T(8,128)(2,1)} async-done(((bf16[512,768]{1,0:T(8,128)(2,1)}), bf16[2048,768]{1,0:T(8,128)(2,1)}) %all-gather.9.cloned.1.call-update) | async-done | bytes 3145744 | tf_op jit(solution)/shard_map/all_gather | solution.py:133
  76.6 3.1 fusion.53
  80.4 3.2 convolution_convert_fusion.4
  84.9 39.1 %while.28 = (s32[]{:T(128)}, bf16[4,512,3,64]{1,3,2,0:T(8,128)(2,1)S(1)}, f32[4,3,512]{2,1,0:T(4,128)}, bf16[4,512,3,64]{1,3,2,0:T(8,128)(2,1)S(1)}, bf16[2048,3...) while((s32[]{:T(128)}, ...), condition=%wide.region_3.4_spmd.clone, body=%wide.region_0.3_spmd.clone.sunk | while | flops 843153920 | bytes 39778412 | solution.py:181
  87.6 2.8 fusion.137
  90.4 3.7 fusion.138
  97.4 2.8 fusion.137
  100.2 3.7 fusion.138
  107.1 2.8 fusion.137
  110.0 3.7 fusion.138
  116.9 2.8 fusion.137
  119.7 3.7 fusion.138
  128.3 58.6 %reduce-scatter.7.cloned.1.call-done = bf16[512,768]{1,0:T(8,128)(2,1)} async-done(((bf16[2048,768]{1,0:T(8,128)(2,1)}), bf16[512,768]{1,0:T(8,128)(2,1)}) %reduce-scatter.7.cloned.1.call-update) | async-done | bytes 786448 | tf_op jit(solution)/shard_map/reduce_scatter | solution.py:183
  193.4 9.1 %all-gather.1 = bf16[8,1,384]{2,1,0:T(2,128)(2,1)S(1)} all-gather(bf16[1,1,384]{2,1,0:T(2,128)(2,1)S(1)} %reshape.157), channel_id=1, replica_groups=mesh['dp'=8,'tensor'=4] {'dp'}, dimensions={0}, use_global_device_ids=true | all-gather | bytes 6912 | tf_op jit(solution)/shard_map/all_gather | solution.py:129
  204.4 51.0 %all-gather.11.cloned.1.call-done = bf16[2048,768]{1,0:T(8,128)(2,1)} async-done(((bf16[512,768]{1,0:T(8,128)(2,1)}), bf16[2048,768]{1,0:T(8,128)(2,1)}) %all-gather.11.cloned.1.call-update) | async-done | bytes 3145744 | tf_op jit(solution)/shard_map/all_gather | solution.py:136
  255.4 19.0 %multiply_convert_fusion.1 = (bf16[2048,768]{1,0:T(8,128)(2,1)}, f32[2048,768]{1,0:T(8,128)}, f32[2048,768]{1,0:T(8,128)}) fusion(f32[768]{0:T(1024)} %dynamic_slice.31, bf16[2048,768]{1,0:T(8,128)(2,1)} %all-gather.11.cloned.1.call-done, bf16[768,768]{1,0:T(8,128)(2,1)} %all-gather.13.cloned.1.call-done), kind=kOutput, calls=%fused_computation.57 | convolution fusion | flops 2519728128 | bytes 20057088 | tf_op jit(solution)/shard_map/dot_general | solution.py:47
  274.4 5.3 all-gather.15.cloned.1.call-done
  279.6 6.5 convolution_convert_fusion.1
  288.7 42.4 %psum.29 = f32[]{:T(128)} all-reduce(f32[]{:T(128)} %get-tuple-element.280), channel_id=1, replica_groups=mesh['dp'=8,'tensor'=4] {'dp','tensor'}, use_global_device_ids=true, to_apply=%region_14.15 | all-reduce | flops 1 | bytes 8 | tf_op jit(solution)/shard_map/psum | solution.py:207
  333.7 14.0 %reduce-scatter.9.cloned.1.call-done = bf16[512,768]{1,0:T(8,128)(2,1)} async-done(((bf16[2048,768]{1,0:T(8,128)(2,1)}), bf16[512,768]{1,0:T(8,128)(2,1)}) %reduce-scatter.9.cloned.1.call-update) | async-done | bytes 786448 | tf_op jit(solution)/shard_map/reduce_scatter | solution.py:196
  356.0 63.0 %all-gather.17.cloned.1.call-done = bf16[2048,768]{1,0:T(8,128)(2,1)} async-done(((bf16[512,768]{1,0:T(8,128)(2,1)}), bf16[2048,768]{1,0:T(8,128)(2,1)}) %all-gather.17.cloned.1.call-update) | async-done | bytes 3145744 | tf_op jit(solution)/shard_map/all_gather | solution.py:225
  419.0 11.1 %convert_reduce_fusion = (f32[768]{0:T(1024)}, bf16[2048,768]{1,0:T(8,128)(2,1)S(1)}) fusion(f32[2048,768]{1,0:T(8,128)} %get-tuple-element.285, f32[2048,768]{1,0:T(8,128)} %get-tuple-element.304, f32[768]{0:T(1024)} %dynamic_slice.31, bf16[2048,768]{1,0:T(8,128)(2,1)} %all-gather.17.cloned.1.call-done, bf16[768,768]{0,1:T(8,128)(2,1)} %all-gather.15.cloned.1.call-done), kind=kOutput, calls=%fused_computation.54 | convolution fusion | flops 2442657024 | bytes 20060160 | tf_op jit(solution)/shard_map/dot_general | solution.py:35
  431.8 4.0 convolution_convert_fusion
  435.9 59.1 %reduce-scatter.11.cloned.1.call-done = bf16[512,768]{1,0:T(8,128)(2,1)} async-done(((bf16[2048,768]{1,0:T(8,128)(2,1)}), bf16[512,768]{1,0:T(8,128)(2,1)}) %reduce-scatter.11.cloned.1.call-update) | async-done | bytes 786448 | tf_op jit(solution)/shard_map/reduce_scatter | solution.py:231
  495.0 3.4 multiply_reduce_fusion.2
  502.2 63.2 %all-gather.19.cloned.1.call-done = bf16[2048,768]{1,0:T(8,128)(2,1)} async-done(((bf16[512,768]{1,0:T(8,128)(2,1)}), bf16[2048,768]{1,0:T(8,128)(2,1)}) %all-gather.19.cloned.1.call-update) | async-done | bytes 3145744 | tf_op jit(solution)/shard_map/all_gather | solution.py:245
  565.4 4.0 convolution_convert_fusion.3
  569.4 3.0 reshape.151
  575.5 109.5 %while.29 = (s32[]{:T(128)}, f32[2048,3,64]{0,2,1:T(8,128)S(1)}, f32[2048,3,64]{0,2,1:T(8,128)}, bf16[4,512,3,64]{1,3,2,0:T(8,128)(2,1)}, bf16[4,512,3,64]{1,3,2...) while((s32[]{:T(128)}, f32[2048,3,64]{0,2,1:T(8,128)S(1)}, ...), condition=%wide.region_22.23_spmd.clone, body=%wide.region_20.22_spmd.clone.sunk | while | flops 2062615040 | bytes 129222840 | solution.py:278
  576.9 2.8 fusion.148
  579.6 4.9 fusion.150
  584.6 4.8 multiply_reduce_fusion.12
  589.4 5.0 multiply_convert_fusion.3
  594.4 5.6 fusion.151
  603.7 2.8 fusion.148
  606.5 5.5 fusion.150
  612.0 4.8 multiply_reduce_fusion.12
  616.9 5.0 multiply_convert_fusion.3
  621.9 5.6 fusion.151
  631.2 2.8 fusion.148
  634.0 5.5 fusion.150
  639.5 4.8 multiply_reduce_fusion.12
  644.4 5.0 multiply_convert_fusion.3
  649.3 5.6 fusion.151
  658.7 2.8 fusion.148
  661.5 5.5 fusion.150
  667.0 4.8 multiply_reduce_fusion.12
  671.9 5.0 multiply_convert_fusion.3
  676.8 5.7 fusion.151
  691.7 2.8 add_convert_fusion
  696.4 6.0 fusion.71
  702.5 7.0 fusion.72
  712.7 3.9 all-to-all-start.1
  716.7 2.9 fusion.58
  719.6 3.1 fusion.59
  727.2 4.2 all-to-all-start
  732.6 45.2 %all-reduce = (f32[]{:T(128)}, f32[8,768]{1,0:T(8,128)S(1)}, f32[3072]{0:T(1024)S(1)}) all-reduce(f32[]{:T(128)} %get-tuple-element.305, f32[8,768]{1,0:T(8,128)S(1)} %stack.74, f32[3072]{0:T(1024)S(1)} %dynamic_update_slice.24), channel_id=1, replica_groups=mesh['dp'=8,'tensor'=4] {'dp','tensor'}, use_global_device_ids=true, to_apply=%region_12.13 | all-reduce | flops 9217 | bytes 73736 | tf_op jit(solution)/shard_map/psum | solution.py:207
  785.1 14.7 %reduce-scatter.15.cloned.1.call-done = f32[96,768]{1,0:T(8,128)} async-done(((f32[768,768]{1,0:T(8,128)}), f32[96,768]{1,0:T(8,128)}) %reduce-scatter.15.cloned.1.call-update) | async-done | bytes 294928 | tf_op jit(solution)/shard_map/reduce_scatter | solution.py:238
  799.8 46.3 %reduce-scatter.17.cloned.1.call-done = f32[768,96]{0,1:T(8,128)} async-done(((f32[768,768]{0,1:T(8,128)}), f32[768,96]{0,1:T(8,128)}) %reduce-scatter.17.cloned.1.call-update) | async-done | bytes 294928 | tf_op jit(solution)/shard_map/reduce_scatter | solution.py:239
  (210 shorter events, 89.7 us)
Async XLA Ops:
  8.0 68.6 %all-gather.9.cloned.1.call-start = ((), (), s32[]{:S(2)}) async-start(), calls=%async_computation.8 | async-start | bytes 3932160 | tf_op jit(solution)/shard_map/all_gather | solution.py:133
  8.8 178.1 %reduce-scatter.7.cloned.1.call-start = ((), (), s32[]{:S(2)}) async-start(), calls=%async_computation.9 | async-start | bytes 3932160 | tf_op jit(solution)/shard_map/reduce_scatter | solution.py:183
  39.4 37.2 %copy-start.20 = (bf16[768,192]{1,0:T(8,128)(2,1)}, bf16[768,192]{1,0:T(8,128)(2,1)S(1)}, u32[]{:S(2)}) copy-start(bf16[768,192]{1,0:T(8,128)(2,1)S(1)} %all_gather.45) | copy-start | bytes 884740
  48.7 31.8 %copy-start.16 = (bf16[768,192]{1,0:T(8,128)(2,1)}, bf16[768,192]{1,0:T(8,128)(2,1)S(1)}, u32[]{:S(2)}) copy-start(bf16[768,192]{1,0:T(8,128)(2,1)S(1)} %all_gather.47) | copy-start | bytes 884740
  57.7 26.0 %copy-start.22 = (bf16[768,192]{1,0:T(8,128)(2,1)}, bf16[768,192]{1,0:T(8,128)(2,1)S(1)}, u32[]{:S(2)}) copy-start(bf16[768,192]{1,0:T(8,128)(2,1)S(1)} %all_gather.48) | copy-start | bytes 884740
  80.3 3.4 copy-start.1
  124.0 0.9 copy-start.5
  124.9 2.8 copy-start.15
  124.9 62.0 %copy-start.3 = (bf16[512,768]{1,0:T(8,128)(2,1)S(1)}, bf16[512,768]{1,0:T(8,128)(2,1)}, u32[]{:S(2)}) copy-start(bf16[512,768]{1,0:T(8,128)(2,1)} %param.24) | copy-start | bytes 2359300
  127.7 76.7 %all-gather.13.cloned.1.call-start = ((), (), s32[]{:S(2)}) async-start(), calls=%async_computation.11 | async-start | bytes 1327104 | tf_op jit(solution)/shard_map/all_gather | solution.py:126
  128.3 127.1 %all-gather.11.cloned.1.call-start = ((), (), s32[]{:S(2)}) async-start(), calls=%async_computation.10 | async-start | bytes 3932160 | tf_op jit(solution)/shard_map/all_gather | solution.py:136
  186.9 3.1 copy-start.4
  192.1 87.6 %all-gather.15.cloned.1.call-start = ((), (), s32[]{:S(2)}) async-start(), calls=%async_computation.12 | async-start | bytes 1327104 | tf_op jit(solution)/shard_map/all_gather | solution.py:127
  192.7 155.0 %reduce-scatter.9.cloned.1.call-start = ((), (), s32[]{:S(2)}) async-start(), calls=%async_computation.13 | async-start | bytes 3932160 | tf_op jit(solution)/shard_map/reduce_scatter | solution.py:196
  286.2 132.8 %all-gather.17.cloned.1.call-start = ((), (), s32[]{:S(2)}) async-start(), calls=%async_computation.14 | async-start | bytes 3932160 | tf_op jit(solution)/shard_map/all_gather | solution.py:225
  347.6 2.3 copy-start.18
  347.6 2.3 copy-start.26
  347.6 4.9 copy-start.33
  347.6 5.5 copy-start.24
  347.6 5.5 copy-start.25
  355.6 139.4 %reduce-scatter.11.cloned.1.call-start = ((), (), s32[]{:S(2)}) async-start(), calls=%async_computation.15 | async-start | bytes 3932160 | tf_op jit(solution)/shard_map/reduce_scatter | solution.py:231
  419.0 12.8 %copy-start.36 = (bf16[768,768]{1,0:T(8,128)(2,1)S(1)}, bf16[768,768]{1,0:T(8,128)(2,1)}, u32[]{:S(2)}) copy-start(bf16[768,768]{1,0:T(8,128)(2,1)} %all-gather.13.cloned.1.call-done) | copy-start | bytes 3538948
  430.1 1.7 copy-start.37
  435.8 129.6 %all-gather.19.cloned.1.call-start = ((), (), s32[]{:S(2)}) async-start(), calls=%async_computation.16 | async-start | bytes 3932160 | tf_op jit(solution)/shard_map/all_gather | solution.py:245
  495.0 3.4 copy-start.8
  495.0 3.4 copy-start.19
  499.7 1.2 copy-start.6
  502.0 280.7 %reduce-scatter.13.cloned.1.call-start = ((), (), s32[]{:S(2)}) async-start(), calls=%async_computation.17 | async-start | bytes 3932160 | tf_op jit(solution)/shard_map/reduce_scatter | solution.py:292
  594.4 5.6 copy-start
  621.9 5.6 copy-start
  649.3 5.6 copy-start
  676.8 5.7 copy-start
  685.2 5.2 copy-start.11
  685.2 4.1 copy-start.17
  687.4 3.0 copy-start.10
  689.3 2.4 copy-start.12
  689.3 1.3 copy-start.21
  690.6 1.1 copy-start.23
  694.5 1.9 copy-start.35
  694.5 105.3 %reduce-scatter.15.cloned.1.call-start = ((), (), s32[]{:S(2)}) async-start(), calls=%async_computation.18 | async-start | bytes 2654208 | tf_op jit(solution)/shard_map/reduce_scatter | solution.py:238
  702.4 7.1 copy-start.9
  702.4 143.7 %reduce-scatter.17.cloned.1.call-start = ((), (), s32[]{:S(2)}) async-start(), calls=%async_computation.19 | async-start | bytes 2654208 | tf_op jit(solution)/shard_map/reduce_scatter | solution.py:239
  712.7 14.4 %all-to-all-start.1 = ((bf16[8,192,96]{2,1,0:T(8,128)(2,1)}), bf16[8,192,96]{2,1,0:T(8,128)(2,1)S(1)}, u32[]{:S(2)}, u32[]{:S(2)}) async-start(bf16[8,192,96]{2,1,0:T(8,128)(2,1)} %bitcast.145), calls=%async_computation.5 | async-start | bytes 786432 | tf_op jit(solution)/shard_map/all_to_all | solution.py:21
  719.6 3.1 copy-start.2
  719.6 3.3 copy-start.13
  723.7 7.7 copy-start.28
  723.7 7.7 copy-start.27
  723.7 7.8 copy-start.34
  723.7 8.1 copy-start.31
  723.8 8.0 copy-start.32
  723.8 8.1 copy-start.30
  723.8 8.1 copy-start.29
  723.8 8.1 copy-start.14
  724.8 57.8 %copy-start.7 = (f32[512,768]{1,0:T(8,128)S(1)}, f32[512,768]{1,0:T(8,128)}, u32[]{:S(2)}) copy-start(f32[512,768]{1,0:T(8,128)} %copy-done.6) | copy-start | bytes 4718596
  727.2 53.3 %all-to-all-start = ((bf16[8,96,576]{2,1,0:T(8,128)(2,1)}), bf16[8,96,576]{2,1,0:T(8,128)(2,1)}, u32[]{:S(2)}, u32[]{:S(2)}) async-start(bf16[8,96,576]{2,1,0:T(8,128)(2,1)} %bitcast.193), calls=%async_computation.4 | async-start | bytes 1966080 | tf_op jit(solution)/shard_map/all_to_all | solution.py:21
Sparse Core Ops, SparseCore 0:
  10.4 66.1 all-gather.8
  127.8 59.0 reduce-scatter.6
  355.7 63.3 all-gather.16
  502.1 63.2 all-gather.18
  694.6 59.0 reduce-scatter.12
  757.5 42.2 reduce-scatter.14
  803.7 42.3 reduce-scatter.16
Sparse Core Ops, SparseCore 1:
  130.1 22.4 all-gather.12
  192.2 63.2 all-gather.10
  257.1 22.4 all-gather.14
  286.3 61.3 reduce-scatter.8
  435.9 59.0 reduce-scatter.10
where the time goes:
time: 860 us; the launch traced here: 855 us
  waiting for transfers between devices  395 us (46%)
  matrix products  188 us (22%)
  blocking collectives  144 us (17%)
  other arithmetic  68.8 us (8%)
  local copies, waits for them, and re-layouts  29.3 us (3%)
  between operations  20.5 us (2%)
  starting transfers between devices  9.25 us (1%)
    psum x2, blocking collectives, shards(): lax.psum((loss_local, count_local), ('dp', 'tensor'))  87.7 us
    all_gather x1, waiting for transfers between devices, shards(): lax.all_gather(grad_first.astype(jnp.bfloat16), 'tensor', axis=0, tiled=T...  63.2 us
    all_gather x1, waiting for transfers between devices, shards(): lax.all_gather(grad_second.astype(jnp.bfloat16), 'tensor', axis=0, tiled=...  63 us
    reduce_scatter x1, waiting for transfers between devices, shards(): lax.psum_scatter(contract_last(grad_pre, inner_full).astype(jnp.bfloat16)...  59.1 us
    reduce_scatter x1, waiting for transfers between devices, shards(): lax.psum_scatter(plain_dot(attended, mixer_full).astype(jnp.bfloat16), 't...  58.6 us
    all_gather x1, waiting for transfers between devices, ffn_gather(): return lax.all_gather(values_in, 'tensor', axis=0, tiled=True)  51 us
    reduce_scatter x1, waiting for transfers between devices, shards(): lax.psum_scatter(outer_local, 'dp', scatter_dimension=1, tiled=True)  46.3 us
    dot_general x6, matrix products, plain_dot(): return jnp.dot(left_rows, right_rows, preferred_element_type=jnp.float32)  35.7 us
  transfers between devices with their start and end apart: 14, of which 10 were waited for; matrix products, arithmetic and copies ran while one was open for 8% of the time, Pallas kernels for 0%

commit v1 on v0

--- a/solution.py
+++ b/solution.py
@@ -1,14 +1,1056 @@
+import functools
 import jax
 import jax.numpy as jnp
 from jax import lax
+from jax.experimental import pallas as pl
+from jax.experimental.pallas import tpu as pltpu
 from jax.sharding import PartitionSpec as P
 
 HEAD_DIM = 64
 QBLOCK = 512
-
-
+MESH = pl.DeviceIdType.MESH
+F32 = jnp.float32
+BF16 = jnp.bfloat16
 norm_eps = 1e-05
 masked_score = -1e30
+VMEM_LIMIT = 60 * 1024 * 1024
+
+
+def dot(left, right, left_dim, right_dim):
+    return lax.dot_general(
+        left, right, (((left_dim,), (right_dim,)), ((), ())), preferred_element_type=F32
+    )
+
+
+def remote(src, dst, send, recv, d, t):
+    return pltpu.make_async_remote_copy(
+        src_ref=src,
+        dst_ref=dst,
+        send_sem=send,
+        recv_sem=recv,
+        device_id={"dp": d, "tensor": t},
+        device_id_type=MESH,
+    )
+
+
+def arrival(dst, recv):
+    return pltpu.make_async_copy(dst, dst, recv)
+
+
+class Place:
+    def __init__(self):
+        self.dp = lax.axis_size("dp")
+        self.tp = lax.axis_size("tensor")
+        self.d = lax.axis_index("dp")
+        self.z = lax.axis_index("tensor")
+        self.core = lax.rem(self.d, 2)
+        self.chip = self.d // 2
+        self.chips = self.dp // 2
+        self.base = self.chip * 2
+        self.sibling = self.base + 1 - self.core
+        self.pair = self.z // 2
+        self.low = lax.rem(self.z, 2)
+        self.group = 2 * self.low + self.core
+        self.buddy = 2 * self.pair + 1 - self.low
+        self.owner = self.base + self.pair
+        self.near_here = 1 + self.pair
+        self.near_there = 2 - self.pair
+
+
+def greet(place):
+    barrier = pltpu.get_barrier_semaphore()
+    count = 0
+    for t in range(place.tp):
+        for c in range(2):
+            other = jnp.logical_not(jnp.logical_and(place.z == t, place.core == c))
+
+            @pl.when(other)
+            def _(t=t, c=c):
+                pl.semaphore_signal(
+                    barrier, inc=1, device_id={"dp": place.base + c, "tensor": t}, device_id_type=MESH
+                )
+
+            count += 1
+    count -= 1
+
+    def plane(i, _):
+        chip = lax.rem(place.chip + 1 + i, place.chips)
+        for c in range(2):
+            pl.semaphore_signal(
+                barrier, inc=1, device_id={"dp": chip * 2 + c, "tensor": place.z}, device_id_type=MESH
+            )
+        return 0
+
+    lax.fori_loop(0, place.chips - 1, plane, 0)
+    count += 2 * (place.chips - 1)
+    pl.semaphore_wait(barrier, count)
+
+
+def front_kernel(
+    x_ref, wq_ref, wm_ref, sm_ref,
+    oin_ref, wall_ref, smalls_ref, count_ref, xs_ref, wqf_ref, oT_ref, lse_ref, qT_ref, kA_ref, v_ref,
+    wqz, counts, vT, scores, o_buf, wqT, wkp, wvp, wvT,
+    sm_send, sm_recv, cn_send, cn_recv, wz_send, wz_recv, wp_send, wp_recv,
+    x_send, x_recv, xr_send, xf_send, mz_send, mz_recv, mp_send, mp_recv, ms_send, ms_recv, o_send, o_recv,
+):
+    me = Place()
+    dp, tp, chips = me.dp, me.tp, me.chips
+    rows, width = x_ref.shape
+    half = rows // 2
+    length = rows * tp
+    share = wq_ref.shape[0]
+    heads = 3
+    greet(me)
+
+    def each_peer(f):
+        def step(i, _):
+            f(i, lax.rem(me.d + 1 + i, dp))
+            return 0
+
+        lax.fori_loop(0, dp - 1, step, 0)
+
+    def small_copy(i, peer):
+        return remote(sm_ref, smalls_ref.at[me.d], sm_send.at[i], sm_recv.at[me.d], peer, me.z)
+
+    each_peer(lambda i, peer: small_copy(i, peer).start())
+    smalls_ref[me.d] = sm_ref[...]
+
+    for s in range(2):
+        target = me.z // 2 + 2 * s
+        src, dst = wq_ref, wqz.at[me.low]
+
+        @pl.when(target == me.z)
+        def _(s=s, dst=dst):
+            pltpu.make_async_copy(wq_ref, dst, wz_recv.at[me.low]).start()
+
+        @pl.when(target != me.z)
+        def _(s=s, dst=dst, target=target):
+            remote(wq_ref, dst, wz_send.at[s], wz_recv.at[me.low], me.d, target).start()
+
+    is_owner = me.core == me.pair
+    for h in range(2):
+        part = pl.ds(h * half, half)
+
+        @pl.when(is_owner)
+        def _(h=h, part=part):
+            pltpu.make_async_copy(x_ref.at[part], xs_ref.at[me.z, part], x_recv.at[me.z, h]).start()
+            remote(x_ref.at[part], xs_ref.at[me.z, part], x_send.at[h], x_recv.at[me.z, h], me.base + h, me.buddy).start()
+            remote(x_ref.at[part], xs_ref.at[me.z, part], xr_send.at[0, h], x_recv.at[me.z, h], me.sibling, me.z).start()
+
+        @pl.when(jnp.logical_not(is_owner))
+        def _(h=h, part=part):
+            remote(x_ref.at[part], xs_ref.at[me.z, part], x_send.at[h], x_recv.at[me.z, h], me.base + h, me.near_there).start()
+
+    pltpu.make_async_copy(wm_ref, wall_ref.at[me.z, me.d], mz_recv.at[me.z]).start()
+    for s in range(1, tp):
+        t = lax.rem(me.z + s, tp)
+        remote(wm_ref, wall_ref.at[me.z, me.d], mz_send.at[s - 1], mz_recv.at[me.z], me.d, t).start()
+
+    def wq_plane(s, k):
+        dst = wqf_ref.at[me.d]
+        return remote(wqz.at[s], dst, wp_send.at[s, k], wp_recv.at[me.d], 2 * k + s, me.z)
+
+    for s in range(2):
+        arrival(wqz.at[s], wz_recv.at[s]).wait()
+
+        def step(i, _, s=s):
+            k = lax.rem(me.chip + 1 + i, chips)
+            here = 2 * k + s == me.d
+
+            @pl.when(here)
+            def _():
+                pltpu.make_async_copy(wqz.at[s], wqf_ref.at[me.d], wp_recv.at[me.d]).start()
+
+            @pl.when(jnp.logical_not(here))
+            def _():
+                wq_plane(s, k).start()
+
+            return 0
+
+        lax.fori_loop(0, chips, step, 0)
+
+    def plane_units(t):
+        def step(i, _):
+            k = lax.rem(me.chip + 1 + i, chips)
+            remote(
+                wall_ref.at[t, me.d], wall_ref.at[t, me.d], mp_send.at[t, i], mp_recv.at[t, me.chip], 2 * k + me.core, me.z
+            ).start()
+            return 0
+
+        lax.fori_loop(0, chips - 1, step, 0)
+
+    arrival(wall_ref.at[me.z, me.d], mz_recv.at[me.z]).wait()
+    plane_units(me.z)
+
+    def small_wait(i, peer):
+        arrival(smalls_ref.at[peer], sm_recv.at[peer]).wait()
+
+    each_peer(small_wait)
+    plane_count = smalls_ref[0][8:16]
+    for k in range(1, dp):
+        plane_count = plane_count + smalls_ref[k][8:16]
+    counts[me.z] = plane_count
+    for s in range(1, tp):
+        remote(counts.at[me.z], counts.at[me.z], cn_send.at[s - 1], cn_recv.at[me.z], me.d, lax.rem(me.z + s, tp)).start()
+
+    for k in range(dp):
+        arrival(wqf_ref.at[k], wp_recv.at[k]).wait()
+    zero = jnp.zeros((share, HEAD_DIM), BF16)
+    gw = heads * HEAD_DIM
+    for k in range(dp):
+        w = wqf_ref[k]
+        at = slice(k * share, (k + 1) * share)
+        pads = []
+        for m in range(3):
+            cols = []
+            for h in range(heads):
+                cols += [w[:, m * gw + h * HEAD_DIM : m * gw + (h + 1) * HEAD_DIM], zero]
+            pads.append(jnp.concatenate(cols, axis=1))
+        wkp[at, :] = pads[1]
+        wvp[at, :] = pads[2]
+        scores[0, at, 0:384] = pads[0].astype(F32)
+    wqT[...] = scores[0, 0:width, 0:384].T.astype(BF16)
+    wvT[...] = wvp[...].astype(F32).T.astype(BF16)
+
+    blocks = gw // share
+    row_bias = jnp.zeros((8, 384), F32)
+    col_bias = jnp.zeros((384, 8), F32)
+    r_in = lax.broadcasted_iota(jnp.int32, (128, 384), 0)
+    r_out = lax.broadcasted_iota(jnp.int32, (128, 384), 1)
+    c_out = lax.broadcasted_iota(jnp.int32, (384, 128), 0)
+    c_in = lax.broadcasted_iota(jnp.int32, (384, 128), 1)
+
+    def padded(col):
+        return (col // HEAD_DIM) * 128 + lax.rem(col, HEAD_DIM)
+
+    for b in range(blocks):
+        vecs = smalls_ref[me.group * blocks + b][0:8].astype(BF16)
+        sel = jnp.logical_and(padded(r_in + b * share) == r_out, r_in < share)
+        row_bias = row_bias + dot(vecs, jnp.where(sel, 1.0, 0.0).astype(BF16), 1, 0)
+        sel = jnp.logical_and(padded(c_in + b * share) == c_out, c_in < share)
+        col_bias = col_bias + dot(jnp.where(sel, 1.0, 0.0).astype(BF16), vecs, 1, 1)
+    q_bias = col_bias[:, 0:1]
+    v_bias_col = col_bias[:, 1:2]
+    v_bias = row_bias[1:2, :]
+    valid = smalls_ref[me.base + me.pair][12:13, 0:1]
+
+    lane = lax.broadcasted_iota(jnp.int32, (rows, 128), 1)
+    srow = lax.broadcasted_iota(jnp.int32, (128, rows), 0)
+
+    def project(j):
+        at = pl.ds(pl.multiple_of(j * rows, rows), rows)
+        xb = xs_ref[j]
+        keys = dot(xb, wkp[...], 1, 0)
+        queries = dot(wqT[...], xb, 1, 1) + q_bias
+        vals = dot(xb, wvp[...], 1, 0) + v_bias
+        valsT = dot(wvT[...], xb, 1, 1) + v_bias_col
+        pos = (j * rows + lax.broadcasted_iota(jnp.int32, (rows, 128), 0)).astype(F32)
+        bias = jnp.where(pos < valid, 0.0, masked_score)
+        for h in range(heads):
+            span = slice(h * 128, (h + 1) * 128)
+            vT[h * HEAD_DIM : (h + 1) * HEAD_DIM, at] = valsT[h * 128 : h * 128 + HEAD_DIM].astype(BF16)
+            kA_ref[h, at, :] = jnp.where(lane == HEAD_DIM, bias, keys[:, span]).astype(BF16)
+            qh = queries[span].astype(BF16) * BF16(HEAD_DIM**-0.5)
+            qT_ref[h, :, at] = jnp.where(srow == HEAD_DIM, BF16(1), qh)
+            v_ref[h, at, :] = vals[:, span].astype(BF16)
+
+    def wait_half(j, h):
+        arrival(xs_ref.at[j, pl.ds(h * half, half)], x_recv.at[j, h]).wait()
+
+    mine = pl.ds(pl.multiple_of(me.core * half, half), half)
+
+    def relay(j, slot):
+        arrival(xs_ref.at[j, mine], x_recv.at[j, me.core]).wait()
+        remote(xs_ref.at[j, mine], xs_ref.at[j, mine], xr_send.at[slot, 0], x_recv.at[j, me.core], me.sibling, me.z).start()
+
+    wait_half(me.z, 0)
+    wait_half(me.z, 1)
+    project(me.z)
+    relay(me.buddy, 1)
+    wait_half(me.buddy, 0) if False else None
+    far_first = 2 * (1 - me.pair) + me.pair
+    far_second = 2 * (1 - me.pair) + 1 - me.pair
+
+    is_near = me.z == me.near_here
+    for n, j in enumerate((far_first, far_second)):
+        relay(j, 2 + n)
+
+        @pl.when(is_near)
+        def _(n=n, j=j):
+            remote(xs_ref.at[j, mine], xs_ref.at[j, mine], xf_send.at[n], x_recv.at[j, me.core], me.d, me.buddy).start()
+
+        if n == 0:
+            arrival(xs_ref.at[me.buddy, pl.ds(pl.multiple_of((1 - me.core) * half, half), half)], x_recv.at[me.buddy, 1 - me.core]).wait()
+            project(me.buddy)
+    for j in (far_first, far_second):
+        arrival(xs_ref.at[j, pl.ds(pl.multiple_of((1 - me.core) * half, half), half)], x_recv.at[j, 1 - me.core]).wait()
+        project(j)
+
+    chunk = 256
+    pieces = length // chunk
+
+    def attend(i, _):
+        j = lax.rem(me.z + 1 + i, tp)
+        at = pl.ds(pl.multiple_of(j * rows, rows), rows)
+        tops = []
+        for h in range(heads):
+            qt = qT_ref[h, :, at]
+            top = None
+            for c in range(pieces):
+                s = dot(kA_ref[h, c * chunk : (c + 1) * chunk, :], qt, 1, 0)
+                scores[h, c * chunk : (c + 1) * chunk, :] = s
+                peak = jnp.max(s, axis=0, keepdims=True)
+                top = peak if top is None else jnp.maximum(top, peak)
+            tops.append(top)
+        outs = []
+        for h in range(heads):
+            total, mixed = None, None
+            for c in range(pieces):
+                p = jnp.exp(scores[h, c * chunk : (c + 1) * chunk, :] - tops[h])
+                part = jnp.sum(p, axis=0, keepdims=True)
+                term = dot(vT[h * HEAD_DIM : (h + 1) * HEAD_DIM, c * chunk : (c + 1) * chunk], p.astype(BF16), 1, 0)
+                total = part if total is None else total + part
+                mixed = term if mixed is None else mixed + term
+            mixed = mixed / total
+            oT_ref[h * HEAD_DIM : (h + 1) * HEAD_DIM, at] = mixed
+            lse_ref[h, :, at] = tops[h] + jnp.log(total)
+            outs.append(mixed)
+        o_buf[j] = jnp.concatenate(outs, axis=0).T.astype(BF16)
+        here = jnp.logical_and(j == me.z, is_owner)
+
+        @pl.when(here)
+        def _():
+            pltpu.make_async_copy(o_buf.at[j], oin_ref.at[me.group], o_recv.at[me.group]).start()
+
+        @pl.when(jnp.logical_not(here))
+        def _():
+            remote(o_buf.at[j], oin_ref.at[me.group], o_send.at[i], o_recv.at[me.group], me.owner, j).start()
+
+        @pl.when(i == 0)
+        def _():
+            for s in range(1, tp):
+                t = lax.rem(me.z + s, tp)
+                arrival(wall_ref.at[t, me.d], mz_recv.at[t]).wait()
+                plane_units(t)
+
+        return 0
+
+    lax.fori_loop(0, tp, attend, 0)
+
+    def to_sibling(t, k):
+        unit = wall_ref.at[t, 2 * k + me.core]
+        return remote(unit, unit, ms_send.at[t, k], ms_recv.at[t, k], me.sibling, me.z)
+
+    def own_units(t, _):
+        to_sibling(t, me.chip).start()
+        return 0
+
+    lax.fori_loop(0, tp, own_units, 0)
+
+    def others(n, _):
+        i, s = n // tp, lax.rem(n, tp)
+        k = lax.rem(me.chip + 1 + i, chips)
+        t = lax.rem(me.z + s, tp)
+        arrival(wall_ref.at[t, 2 * k + me.core], mp_recv.at[t, k]).wait()
+        to_sibling(t, k).start()
+        return 0
+
+    lax.fori_loop(0, (chips - 1) * tp, others, 0)
+
+    for s in range(1, tp):
+        t = lax.rem(me.z + s, tp)
+        arrival(counts.at[t], cn_recv.at[t]).wait()
+    total = counts[0]
+    for t in range(1, tp):
+        total = total + counts[t]
+    count_ref[...] = total
+    for g in range(4):
+        arrival(oin_ref.at[g], o_recv.at[g]).wait()
+
+    def sibling_units(n, _):
+        t, k = n // chips, lax.rem(n, chips)
+        arrival(wall_ref.at[t, 2 * k + 1 - me.core], ms_recv.at[t, k]).wait()
+        to_sibling(t, k).wait_send()
+        return 0
+
+    lax.fori_loop(0, tp * chips, sibling_units, 0)
+
+    def sent(n, _):
+        t, i = n // (chips - 1), lax.rem(n, chips - 1)
+        remote(wall_ref.at[t, me.d], wall_ref.at[t, me.d], mp_send.at[t, i], mp_recv.at[t, 0], me.sibling, me.z).wait_send()
+        return 0
+
+    lax.fori_loop(0, tp * (chips - 1), sent, 0)
+    each_peer(lambda i, peer: small_copy(i, peer).wait_send())
+    for s in range(2):
+
+        @pl.when(me.z // 2 + 2 * s != me.z)
+        def _(s=s):
+            remote(wq_ref, wqz.at[0], wz_send.at[s], wz_recv.at[0], me.sibling, me.z).wait_send()
+
+        def step(i, _, s=s):
+            k = lax.rem(me.chip + 1 + i, chips)
+
+            @pl.when(2 * k + s != me.d)
+            def _():
+                wq_plane(s, k).wait_send()
+
+            return 0
+
+        lax.fori_loop(0, chips, step, 0)
+    for s in range(tp - 1):
+        remote(counts.at[0], counts.at[0], cn_send.at[s], cn_recv.at[0], me.sibling, me.z).wait_send()
+        remote(wm_ref, wall_ref.at[0, 0], mz_send.at[s], mz_recv.at[0], me.sibling, me.z).wait_send()
+
+    def x_sent(sem):
+        remote(x_ref.at[pl.ds(0, half)], xs_ref.at[0, pl.ds(0, half)], sem, x_recv.at[0, 0], me.sibling, me.z).wait_send()
+
+    for h in range(2):
+        x_sent(x_send.at[h])
+
+        @pl.when(is_owner)
+        def _(h=h):
+            x_sent(xr_send.at[0, h])
+
+    for n in range(3):
+        x_sent(xr_send.at[1 + n, 0])
+
+    @pl.when(is_near)
+    def _():
+        for n in range(2):
+            x_sent(xf_send.at[n])
+
+    def o_sent(i, _):
+        j = lax.rem(me.z + 1 + i, tp)
+
+        @pl.when(jnp.logical_not(jnp.logical_and(j == me.z, is_owner)))
+        def _():
+            remote(o_buf.at[0], oin_ref.at[0], o_send.at[i], o_recv.at[0], me.sibling, me.z).wait_send()
+
+        return 0
+
+    lax.fori_loop(0, tp, o_sent, 0)
+
+
+def front(x, wq, wm, small, dp, tp):
+    rows, width = x.shape
+    length = rows * tp
+    share = wq.shape[0]
+    chips = dp // 2
+    S = jax.ShapeDtypeStruct
+    vmem = pl.BlockSpec(memory_space=pltpu.VMEM)
+    anym = pl.BlockSpec(memory_space=pl.ANY)
+    dma = pltpu.SemaphoreType.DMA
+    return pl.pallas_call(
+        front_kernel,
+        name="front",
+        out_shape=(
+            S((4, rows, 192), BF16),
+            S((tp, dp, share, wm.shape[1]), BF16),
+            S((dp, 16, 128), F32),
+            S((8, 128), F32),
+            S((tp, rows, width), BF16),
+            S((dp, share, wq.shape[1]), BF16),
+            S((192, length), F32),
+            S((3, 1, length), F32),
+            S((3, 128, length), BF16),
+            S((3, length, 128), BF16),
+            S((3, length, 128), BF16),
+        ),
+        in_specs=[vmem, vmem, anym, vmem],
+        out_specs=(anym, anym) + (vmem,) * 9,
+        scratch_shapes=[
+            pltpu.VMEM((2, share, wq.shape[1]), BF16),
+            pltpu.VMEM((tp, 8, 128), F32),
+            pltpu.VMEM((192, length), BF16),
+            pltpu.VMEM((3, length, rows), F32),
+            pltpu.VMEM((tp, rows, 192), BF16),
+            pltpu.VMEM((384, width), BF16),
+            pltpu.VMEM((width, 384), BF16),
+            pltpu.VMEM((width, 384), BF16),
+            pltpu.VMEM((384, width), BF16),
+            dma((dp - 1,)), dma((dp,)), dma((tp - 1,)), dma((tp,)),
+            dma((2,)), dma((2,)), dma((2, chips)), dma((dp,)),
+            dma((2,)), dma((tp, 2)), dma((4, 2)), dma((2,)),
+            dma((tp - 1,)), dma((tp,)), dma((tp, chips - 1)), dma((tp, chips)), dma((tp, chips)), dma((tp, chips)),
+            dma((tp,)), dma((4,)),
+        ],
+        compiler_params=pltpu.CompilerParams(
+            collective_id=0, has_side_effects=True, vmem_limit_bytes=VMEM_LIMIT
+        ),
+    )(x, wq, wm, small)
+
+
+SQRT_HALF = 0.7071067811865476
+INV_SQRT_2PI = 0.3989422804014327
+
+
+def norm_forward(values, gain, shift):
+    centred = values - jnp.mean(values, axis=1, keepdims=True)
+    inv = lax.rsqrt(jnp.mean(centred * centred, axis=1, keepdims=True) + norm_eps)
+    normed = centred * inv
+    return normed * gain + shift, normed, inv
+
+
+def norm_backward(grad_out, normed, inv, gain):
+    g = grad_out * gain
+    plain = jnp.mean(g, axis=1, keepdims=True)
+    mixed = jnp.mean(g * normed, axis=1, keepdims=True)
+    return inv * (g - plain - normed * mixed)
+
+
+def column_sum(values):
+    return jnp.sum(values, axis=0, keepdims=True)
+
+
+def mid_kernel(
+    x_ref, teacher_ref, counted_ref, scale_ref, oin_ref, wall_ref, vec_ref, ib_ref,
+    out_ref, dr1_ref, do_ref, grad_ref, small_ref, ismall_ref,
+    up_ref, act_ref, f_ref, n1_ref, acc_ref, hT_ref, dfT_ref,
+):
+    groups = wall_ref.shape[0]
+    width = x_ref.shape[1]
+    gw = oin_ref.shape[2]
+    inner = slice(0, width)
+    outer = slice(width, 2 * width)
+    mixer = slice(2 * width, 2 * width + gw)
+    vec = lambda i: vec_ref[i : i + 1, :]
+
+    acc_ref[...] = x_ref[...].astype(F32) + vec(2)
+    for g in range(groups):
+        acc_ref[...] += dot(oin_ref[g], wall_ref[g, :, mixer], 1, 1)
+    hidden, normed1, inv1 = norm_forward(acc_ref[...], vec(3), vec(4))
+    n1_ref[...] = normed1
+    low = hidden.astype(BF16)
+    hT_ref[...] = hidden.T.astype(BF16)
+    f_ref[...] = hidden + vec(5)
+
+    def ffn_forward(g, _):
+        up = dot(low, wall_ref[g, :, inner], 1, 0) + ib_ref[g]
+        up_ref[g] = up
+        act = (up * (0.5 * (1.0 + lax.erf(up * SQRT_HALF)))).astype(BF16)
+        act_ref[g] = act
+        f_ref[...] += dot(act, wall_ref[g, :, outer], 1, 1)
+        return 0
+
+    lax.fori_loop(0, groups, ffn_forward, 0)
+    final, normed2, inv2 = norm_forward(f_ref[...], vec(6), vec(7))
+    out_ref[...] = final.astype(BF16)
+    diff = final - teacher_ref[...].astype(F32)
+    counted = counted_ref[...]
+    small_ref[...] = jnp.zeros_like(small_ref)
+    small_ref[6:7, 0:1] = jnp.sum(counted * jnp.sum(diff * diff, axis=1, keepdims=True), axis=0, keepdims=True)
+    grad = (scale_ref[0, 0] * counted) * diff
+    small_ref[4:5, :] = column_sum(grad * normed2)
+    small_ref[5:6, :] = column_sum(grad)
+    dr2 = norm_backward(grad, normed2, inv2, vec(6))
+    small_ref[3:4, :] = column_sum(dr2)
+    acc_ref[...] = dr2
+    df = dr2.astype(BF16)
+    dfT_ref[...] = dr2.T.astype(BF16)
+
+    def ffn_backward(g, _):
+        up = up_ref[g]
+        slope = 0.5 * (1.0 + lax.erf(up * SQRT_HALF)) + up * (INV_SQRT_2PI * jnp.exp(-0.5 * up * up))
+        du = (dot(df, wall_ref[g, :, outer], 1, 0) * slope).astype(BF16)
+        ismall_ref[g] = column_sum(du.astype(F32))
+        acc_ref[...] += dot(du, wall_ref[g, :, inner], 1, 1)
+        grad_ref[g, :, inner] = dot(hT_ref[...], du, 1, 0).astype(BF16)
+        grad_ref[g, :, outer] = dot(dfT_ref[...], act_ref[g], 1, 0).astype(BF16)
+        return 0
+
+    lax.fori_loop(0, groups, ffn_backward, 0)
+    dh1 = acc_ref[...]
+    normed1 = n1_ref[...]
+    small_ref[1:2, :] = column_sum(dh1 * normed1)
+    small_ref[2:3, :] = column_sum(dh1)
+    dr1 = norm_backward(dh1, normed1, inv1, vec(3))
+    small_ref[0:1, :] = column_sum(dr1)
+    dr1_ref[...] = dr1
+    da = dr1.astype(BF16)
+    daT = dr1.T.astype(BF16)
+    for g in range(groups):
+        do_ref[g] = dot(da, wall_ref[g, :, mixer], 1, 0).astype(BF16)
+        grad_ref[g, :, mixer] = dot(daT, oin_ref[g], 1, 0).astype(BF16)
+
+
+def mid(x, teacher, counted, scale, oin, wall, vecs, ib):
+    rows, width = x.shape
+    groups = wall.shape[0]
+    S = jax.ShapeDtypeStruct
+    vmem = pl.BlockSpec(memory_space=pltpu.VMEM)
+    return pl.pallas_call(
+        mid_kernel,
+        name="mid",
+        out_shape=(
+            S((rows, width), BF16),
+            S((rows, width), F32),
+            S(oin.shape, BF16),
+            S(wall.shape, BF16),
+            S((8, width), F32),
+            S(ib.shape, F32),
+        ),
+        in_specs=[vmem, vmem, vmem, pl.BlockSpec(memory_space=pltpu.SMEM)] + [vmem] * 4,
+        out_specs=(vmem,) * 6,
+        scratch_shapes=[
+            pltpu.VMEM((groups, rows, ib.shape[2]), F32),
+            pltpu.VMEM((groups, rows, ib.shape[2]), BF16),
+            pltpu.VMEM((rows, width), F32),
+            pltpu.VMEM((rows, width), F32),
+            pltpu.VMEM((rows, width), F32),
+            pltpu.VMEM((width, rows), BF16),
+            pltpu.VMEM((width, rows), BF16),
+        ],
+        compiler_params=pltpu.CompilerParams(vmem_limit_bytes=VMEM_LIMIT),
+    )(x, teacher, counted, scale, oin, wall, vecs, ib)
+
+
+def back_kernel(
+    do_ref, grad_ref, xs_ref, wqf_ref, oT_ref, lse_ref, qT_ref, kA_ref, v_ref, pack_ref, dr1_ref,
+    dx_ref, gsum_ref, qgrad_ref, small_ref,
+    dof, doT, delta, qs, kT, dk, dv, dqT, dqkv,
+    sib, own, pln, zsrc, zrecv, parts, pr, sj, rr, fin, qsend, qr, qz, qf, spack, srecv, zpack,
+    do_send, do_recv, sb_send, sb_recv, own_sem, pl_send, pl_recv, zz_send, zz_recv,
+    pr_send, pr_recv, rr_send, rr_recv, fin_send, fin_recv, qr_send, qr_recv, qf_send, qf_recv,
+    sm_send, sm_recv, sz_send, sz_recv,
+):
+    me = Place()
+    dp, tp, chips = me.dp, me.tp, me.chips
+    rows, width = dx_ref.shape
+    half = rows // 2
+    length = rows * tp
+    heads = 3
+    gw = heads * HEAD_DIM
+    share = width // dp
+    greet(me)
+
+    for g in range(4):
+        t = 2 * me.core + g // 2
+        d = me.base + g % 2
+        here = jnp.logical_and(t == me.z, g % 2 == me.core)
+
+        @pl.when(here)
+        def _(g=g):
+            pltpu.make_async_copy(do_ref.at[g], dof.at[me.z], do_recv.at[me.z]).start()
+
+        @pl.when(jnp.logical_not(here))
+        def _(g=g, t=t, d=d):
+            remote(do_ref.at[g], dof.at[me.z], do_send.at[g], do_recv.at[me.z], d, t).start()
+
+    def sib_copy(t):
+        return remote(grad_ref.at[t, :, 1 - me.core], sib.at[t], sb_send.at[t], sb_recv.at[t], me.sibling, me.z)
+
+    for t in range(tp):
+        sib_copy(t).start()
+        pltpu.make_async_copy(grad_ref.at[t, :, me.core], own.at[t], own_sem.at[t]).start()
+
+    def pair_sum(t, _):
+        arrival(own.at[t], own_sem.at[t]).wait()
+        arrival(sib.at[t], sb_recv.at[t]).wait()
+
+        def unit(k, _):
+            own[t, k] = (own[t, k].astype(F32) + sib[t, k].astype(F32)).astype(BF16)
+            return 0
+
+        lax.fori_loop(0, chips, unit, 0)
+        return 0
+
+    lax.fori_loop(0, tp, pair_sum, 0)
+
+    def plane_copy(i, t):
+        k = lax.rem(me.chip + 1 + i, chips)
+        return remote(own.at[t, k], pln.at[t, i], pl_send.at[t, i], pl_recv.at[t, i], 2 * k + me.core, me.z)
+
+    def plane_start(n, _):
+        plane_copy(n // tp, lax.rem(n, tp)).start()
+        return 0
+
+    lax.fori_loop(0, (chips - 1) * tp, plane_start, 0)
+
+    def prepare(i, _):
+        j = lax.rem(me.z + i, tp)
+        at = pl.ds(pl.multiple_of(j * rows, rows), rows)
+        arrival(dof.at[j], do_recv.at[j]).wait()
+        flipped = dof[j].astype(F32).T
+        doT[:, at] = flipped.astype(BF16)
+        for h in range(heads):
+            span = slice(h * HEAD_DIM, (h + 1) * HEAD_DIM)
+            delta[h, :, at] = jnp.sum(flipped[span] * oT_ref[span, at], axis=0, keepdims=True)
+            qs[h, at, :] = qT_ref[h, :, at].astype(F32).T.astype(BF16)
+            kT[h, :, at] = kA_ref[h, at, :].astype(F32).T[0:HEAD_DIM, :].astype(BF16)
+        return 0
+
+    lax.fori_loop(0, tp, prepare, 0)
+    chunk = 256
+    for h in range(heads):
+        dk[...] = jnp.zeros_like(dk)
+        dv[...] = jnp.zeros_like(dv)
+
+        def attend(j, _, h=h):
+            at = pl.ds(pl.multiple_of(j * rows, rows), rows)
+            span = slice(h * HEAD_DIM, (h + 1) * HEAD_DIM)
+            qt, gt = qT_ref[h, :, at], doT[span, at]
+            q, go = qs[h, at, :], dof[j, :, span]
+            lse, dl = lse_ref[h, :, at], delta[h, :, at]
+            dq = None
+            for c in range(length // chunk):
+                r = slice(c * chunk, (c + 1) * chunk)
+                p = jnp.exp(dot(kA_ref[h, r, :], qt, 1, 0) - lse)
+                dp_ = dot(v_ref[h, r, 0:HEAD_DIM], gt, 1, 0)
+                ds = (p * (dp_ - dl)).astype(BF16)
+                dv[r, :] += dot(p.astype(BF16), go, 1, 0)
+                dk[r, :] += dot(ds, q, 1, 0)
+                term = dot(kT[h, :, r], ds, 1, 0)
+                dq = term if dq is None else dq + term
+            dqT[span, at] = dq * HEAD_DIM**-0.5
+            return 0
+
+        lax.fori_loop(0, tp, attend, 0)
+        for j in range(tp):
+            at = slice(j * rows, (j + 1) * rows)
+            dqkv[j, :, gw + h * HEAD_DIM : gw + (h + 1) * HEAD_DIM] = dk[at, 0:HEAD_DIM].astype(BF16)
+            dqkv[j, :, 2 * gw + h * HEAD_DIM : 2 * gw + (h + 1) * HEAD_DIM] = dv[at, :].astype(BF16)
+
+    weights = wqf_ref[...].reshape(width, 3 * gw)
+    ones = jnp.ones((8, rows), BF16)
+    mine = pl.ds(pl.multiple_of(me.core * half, half), half)
+    other = pl.ds(pl.multiple_of((1 - me.core) * half, half), half)
+    far = 2 * (1 - me.pair)
+
+    def block_at(i):
+        return jnp.where(i < 2, far + i, jnp.where(i == 2, me.buddy, me.z))
+
+    def pr_copy(j):
+        return remote(parts.at[j, other], pr.at[j], pr_send.at[j], pr_recv.at[j], me.sibling, me.z)
+
+    def token_grads(i, sums):
+        j = block_at(i)
+        at = pl.ds(pl.multiple_of(j * rows, rows), rows)
+        dqkv[j, :, 0:gw] = dqT[:, at].T.astype(BF16)
+        flat = dqkv[j]
+        parts[j] = dot(flat, weights, 1, 1).astype(BF16)
+        pr_copy(j).start()
+        return sums + dot(ones, flat, 1, 0)
+
+    sums = lax.fori_loop(0, tp, token_grads, jnp.zeros((8, 3 * gw), F32))
+
+    spack[...] = pack_ref[...]
+    blocks = gw // share
+    for b in range(blocks):
+        spack[me.group * blocks + b, 0:1, 0:share] = sums[0:1, b * share : (b + 1) * share]
+        spack[me.group * blocks + b, 1:2, 0:share] = sums[0:1, 2 * gw + b * share : 2 * gw + (b + 1) * share]
+
+    def small_copy(i):
+        peer = lax.rem(me.d + 1 + i, dp)
+        return remote(spack.at[peer], srecv.at[i], sm_send.at[i], sm_recv.at[i], peer, me.z)
+
+    def small_start(i, _):
+        small_copy(i).start()
+        return 0
+
+    lax.fori_loop(0, dp - 1, small_start, 0)
+
+    def rr_copy(j):
+        return remote(sj.at[j], rr.at[j], rr_send.at[j], rr_recv.at[j], me.d, me.buddy)
+
+    def collects(j):
+        return jnp.where(j // 2 == me.pair, j, me.near_here) == me.z
+
+    def chip_sum(i, _):
+        j = block_at(i)
+        arrival(pr.at[j], pr_recv.at[j]).wait()
+        sj[j] = (parts[j, mine, :].astype(F32) + pr[j].astype(F32)).astype(BF16)
+
+        @pl.when(jnp.logical_not(collects(j)))
+        def _():
+            rr_copy(j).start()
+
+        return 0
+
+    lax.fori_loop(0, tp, chip_sum, 0)
+
+    def fin_copy(j):
+        return remote(pr.at[j], fin.at[me.core], fin_send.at[j], fin_recv.at[me.core], me.owner, j)
+
+    def lands_here(j):
+        return jnp.logical_and(me.core == me.pair, j == me.z)
+
+    total = None
+    for j in range(tp):
+        term = dot(xs_ref[j], dqkv[j], 0, 0)
+        total = term if total is None else total + term
+    qsend[...] = total.astype(BF16).reshape(dp, share, 3 * gw)
+
+    def q_copy(peer, i):
+        return remote(qsend.at[peer], qr.at[me.core, me.chip], qr_send.at[i], qr_recv.at[me.core, me.chip], peer, me.z)
+
+    def q_start(i, _):
+        peer = lax.rem(me.d + i, dp)
+
+        @pl.when(i == 0)
+        def _():
+            pltpu.make_async_copy(qsend.at[peer], qr.at[me.core, me.chip], qr_recv.at[me.core, me.chip]).start()
+
+        @pl.when(i > 0)
+        def _():
+            q_copy(peer, i).start()
+
+        return 0
+
+    lax.fori_loop(0, dp, q_start, 0)
+
+    def pair_total(i, _):
+        j = block_at(i)
+
+        @pl.when(collects(j))
+        def _():
+            arrival(rr.at[j], rr_recv.at[j]).wait()
+            pr[j] = (sj[j].astype(F32) + rr[j].astype(F32)).astype(BF16)
+
+            @pl.when(lands_here(j))
+            def _():
+                pltpu.make_async_copy(pr.at[j], fin.at[me.core], fin_recv.at[me.core]).start()
+
+            @pl.when(jnp.logical_not(lands_here(j)))
+            def _():
+                fin_copy(j).start()
+
+        return 0
+
+    lax.fori_loop(0, tp, pair_total, 0)
+
+    def plane_total(t, _):
+        total = own[t, me.chip].astype(F32)
+        for i in range(chips - 1):
+            arrival(pln.at[t, i], pl_recv.at[t, i]).wait()
+            total = total + pln[t, i].astype(F32)
+        zsrc[t] = total.astype(BF16)
+        return 0
+
+    lax.fori_loop(0, tp, plane_total, 0)
+
+    def z_copy(s):
+        t = lax.rem(me.z + s, tp)
+        return remote(zsrc.at[t], zrecv.at[s - 1], zz_send.at[s - 1], zz_recv.at[s - 1], me.d, t)
+
+    for s in range(1, tp):
+        z_copy(s).start()
+
+    def q_pair(s):
+        return me.z // 2, 2 * me.low + s
+
+    for s in range(2):
+        total = None
+        for k in range(chips):
+            arrival(qr.at[s, k], qr_recv.at[s, k]).wait()
+            term = qr[s, k].astype(F32)
+            total = term if total is None else total + term
+        qz[s] = total.astype(BF16)
+        p, t = q_pair(s)
+
+        @pl.when(t == me.z)
+        def _(s=s, p=p):
+            pltpu.make_async_copy(qz.at[s], qf.at[p], qf_recv.at[p]).start()
+
+        @pl.when(t != me.z)
+        def _(s=s, p=p, t=t):
+            remote(qz.at[s], qf.at[p], qf_send.at[s], qf_recv.at[p], me.d, t).start()
+
+    total = spack[me.d]
+    for i in range(dp - 1):
+        arrival(srecv.at[i], sm_recv.at[i]).wait()
+        total = total + srecv[i]
+    zpack[me.z] = total
+
+    def sz_copy(s):
+        return remote(zpack.at[me.z], zpack.at[me.z], sz_send.at[s - 1], sz_recv.at[me.z], me.d, lax.rem(me.z + s, tp))
+
+    for s in range(1, tp):
+        sz_copy(s).start()
+
+    for h in range(2):
+        arrival(fin.at[h], fin_recv.at[h]).wait()
+        at = slice(h * half, (h + 1) * half)
+        dx_ref[at, :] = dr1_ref[at, :] + fin[h].astype(F32)
+    for p in range(2):
+        arrival(qf.at[p], qf_recv.at[p]).wait()
+    qgrad_ref[...] = qf[0].astype(F32) + qf[1].astype(F32)
+    for s in range(1, tp):
+        t = lax.rem(me.z + s, tp)
+        arrival(zpack.at[t], sz_recv.at[t]).wait()
+    total = zpack[0]
+    for t in range(1, tp):
+        total = total + zpack[t]
+    small_ref[...] = total
+    total = zsrc[me.z].astype(F32)
+    for s in range(tp - 1):
+        arrival(zrecv.at[s], zz_recv.at[s]).wait()
+        total = total + zrecv[s].astype(F32)
+    gsum_ref[...] = total
+
+    for g in range(4):
+
+        @pl.when(jnp.logical_not(jnp.logical_and(2 * me.core + g // 2 == me.z, g % 2 == me.core)))
+        def _(g=g):
+            remote(do_ref.at[g], dof.at[0], do_send.at[g], do_recv.at[0], me.sibling, me.z).wait_send()
+
+    for t in range(tp):
+        sib_copy(t).wait_send()
+        pr_copy(t).wait_send()
+
+        @pl.when(jnp.logical_not(collects(t)))
+        def _(t=t):
+            rr_copy(t).wait_send()
+
+        @pl.when(jnp.logical_and(collects(t), jnp.logical_not(lands_here(t))))
+        def _(t=t):
+            fin_copy(t).wait_send()
+
+    def plane_sent(n, _):
+        plane_copy(n // tp, lax.rem(n, tp)).wait_send()
+        return 0
+
+    lax.fori_loop(0, (chips - 1) * tp, plane_sent, 0)
+
+    def peers_sent(i, _):
+        small_copy(i).wait_send()
+        q_copy(lax.rem(me.d + 1 + i, dp), i + 1).wait_send()
+        return 0
+
+    lax.fori_loop(0, dp - 1, peers_sent, 0)
+    for s in range(1, tp):
+        z_copy(s).wait_send()
+        sz_copy(s).wait_send()
+    for s in range(2):
+        p, t = q_pair(s)
+
+        @pl.when(t != me.z)
+        def _(s=s, p=p, t=t):
+            remote(qz.at[s], qf.at[p], qf_send.at[s], qf_recv.at[p], me.d, t).wait_send()
+
+
+def back(do, grad, xs, wqf, oT, lse, qT, kA, v, pack, dr1):
+    tp, rows, width = xs.shape
+    dp, share, qwidth = wqf.shape
+    chips = dp // 2
+    length = rows * tp
+    half = rows // 2
+    cols = grad.shape[-1]
+    S = jax.ShapeDtypeStruct
+    vmem = pl.BlockSpec(memory_space=pltpu.VMEM)
+    anym = pl.BlockSpec(memory_space=pl.ANY)
+    dma = pltpu.SemaphoreType.DMA
+    V = pltpu.VMEM
+    return pl.pallas_call(
+        back_kernel,
+        name="back",
+        out_shape=(
+            S((rows, width), F32),
+            S((share, cols), F32),
+            S((share, qwidth), F32),
+            S((16, 128), F32),
+        ),
+        in_specs=[anym, anym] + [vmem] * 9,
+        out_specs=(vmem,) * 4,
+        scratch_shapes=[
+            V((tp, rows, 192), BF16), V((192, length), BF16), V((3, 1, length), F32),
+            V((3, length, 128), BF16), V((3, HEAD_DIM, length), BF16),
+            V((length, 128), F32), V((length, HEAD_DIM), F32), V((192, length), F32), V((tp, rows, qwidth), BF16),
+            V((tp, chips, share, cols), BF16), V((tp, chips, share, cols), BF16), V((tp, chips - 1, share, cols), BF16),
+            V((tp, share, cols), BF16), V((tp - 1, share, cols), BF16),
+            V((tp, rows, width), BF16), V((tp, half, width), BF16), V((tp, half, width), BF16), V((tp, half, width), BF16),
+            V((2, half, width), BF16),
+            V((dp, share, qwidth), BF16), V((2, chips, share, qwidth), BF16), V((2, share, qwidth), BF16), V((2, share, qwidth), BF16),
+            V((dp, 16, 128), F32), V((dp - 1, 16, 128), F32), V((tp, 16, 128), F32),
+            dma((4,)), dma((tp,)), dma((tp,)), dma((tp,)), dma((tp,)), dma((tp, chips - 1)), dma((tp, chips - 1)), dma((tp - 1,)), dma((tp - 1,)),
+            dma((tp,)), dma((tp,)), dma((tp,)), dma((tp,)), dma((tp,)), dma((2,)), dma((dp,)), dma((2, chips)), dma((2,)), dma((2,)),
+            dma((dp - 1,)), dma((dp - 1,)), dma((tp - 1,)), dma((tp,)),
+        ],
+        compiler_params=pltpu.CompilerParams(
+            collective_id=1, has_side_effects=True, vmem_limit_bytes=VMEM_LIMIT
+        ),
+    )(do, grad, xs, wqf, oT, lse, qT, kA, v, pack, dr1)
+
+
+def shards(
+    tokens, teacher, lengths, loss_mask, loss_scale,
+    query_weight, query_bias, key_weight, value_weight, value_bias, mixer_weight, mixer_bias,
+    first_gain, first_shift, inner_weight, inner_bias, outer_weight, outer_bias, second_gain, second_shift,
+):
+    dp, tp = lax.axis_size("dp"), lax.axis_size("tensor")
+    if query_weight.shape[0] % 16 or tp != 4:
+        return plain_shards(
+            tokens, teacher, lengths, loss_mask, loss_scale,
+            query_weight, query_bias, key_weight, value_weight, value_bias, mixer_weight, mixer_bias,
+            first_gain, first_shift, inner_weight, inner_bias, outer_weight, outer_bias, second_gain, second_shift,
+        )
+    z = lax.axis_index("tensor")
+    rows, width = tokens.shape
+    share = query_weight.shape[0]
+    gw = query_weight.shape[1]
+    hidden = inner_weight.shape[1]
+    hshare = inner_bias.shape[0]
+    hrows = -(-hshare // 128)
+    pos = z * rows + jnp.arange(rows)
+    counted = jnp.logical_and(pos < lengths[0], loss_mask == 1).astype(F32)
+    vectors = jnp.stack(
+        [query_bias, value_bias, mixer_bias, first_gain, first_shift, outer_bias, second_gain, second_shift]
+    ).astype(F32)
+    small = jnp.concatenate(
+        [
+            jnp.pad(vectors, ((0, 0), (0, 128 - share))),
+            jnp.full((1, 128), jnp.sum(counted)),
+            jnp.pad(inner_bias.astype(F32), (0, hrows * 128 - hshare)).reshape(hrows, 128),
+            jnp.zeros((3 - hrows, 128), F32),
+            jnp.full((1, 128), lengths[0].astype(F32)),
+            jnp.zeros((3, 128), F32),
+        ],
+        axis=0,
+    )
+    wq = jnp.concatenate([query_weight, key_weight, value_weight], axis=1)
+    wm = jnp.concatenate([inner_weight, outer_weight.T, mixer_weight.T], axis=1)
+    oin, wall, smalls, count, xs, wqf, oT, lse, qT, kA, v = front(tokens, wq, wm, small, dp, tp)
+    token_total = count[0, 0]
+    vecs = jnp.moveaxis(smalls[:, 0:8, 0:share], 0, 1).reshape(8, width)
+    ib = smalls[:, 9 : 9 + hrows, :].reshape(dp, hrows * 128)[:, :hshare].reshape(tp, 1, hidden)
+    scale = (2.0 * loss_scale / (token_total * width)).reshape(1, 1)
+    wall = wall.reshape(tp, width, wm.shape[1])
+    layer_output, dr1, do, grad, sums, isums = mid(tokens, teacher, counted[:, None], scale, oin, wall, vecs, ib)
+    pack = jnp.concatenate(
+        [
+            jnp.zeros((dp, 2, 128), F32),
+            jnp.pad(jnp.moveaxis(sums[0:6].reshape(6, dp, share), 1, 0), ((0, 0), (0, 0), (0, 128 - share))),
+            jnp.broadcast_to(sums[6, 0], (dp, 1, 128)),
+            jnp.pad(isums.reshape(dp, hshare), ((0, 0), (0, hrows * 128 - hshare))).reshape(dp, hrows, 128),
+            jnp.zeros((dp, 7 - hrows, 128), F32),
+        ],
+        axis=1,
+    )
+    grad = grad.reshape(tp, dp // 2, 2, share, wm.shape[1])
+    input_grad, gsum, qgrad, ssum = back(do, grad, xs, wqf, oT, lse, qT, kA, v, pack, dr1)
+    loss_value = ssum[8, 0] / (token_total * width)
+    line = lambda i: ssum[i, :share]
+    innerbias_grad = ssum[9 : 9 + hrows].reshape(-1)[:hshare]
+    return (
+        layer_output,
+        loss_value,
+        input_grad,
+        qgrad[:, 0:gw],
+        line(0),
+        qgrad[:, gw : 2 * gw],
+        qgrad[:, 2 * gw :],
+        line(1),
+        gsum[:, 2 * hidden :].T,
+        line(2),
+        line(3),
+        line(4),
+        gsum[:, 0:hidden],
+        innerbias_grad,
+        gsum[:, hidden : 2 * hidden].T,
+        line(5),
+        line(6),
+        line(7),
+    )
 
 
 def in_blocks(value, dim, size):
@@ -51,14 +1093,14 @@
     return jax.nn.gelu(pre_values, approximate=False)
 
 
-def norm_forward(values_in, gain_vec, shift_vec):
+def plain_norm_forward(values_in, gain_vec, shift_vec):
     centred = values_in - jnp.mean(values_in, axis=1, keepdims=True)
     inv_std = lax.rsqrt(jnp.mean(centred * centred, axis=1, keepdims=True) + norm_eps)
     normed = centred * inv_std
     return (normed * gain_vec + shift_vec, normed, inv_std)
 
 
-def norm_backward(grad_out, normed, inv_std, gain_vec):
+def plain_norm_backward(grad_out, normed, inv_std, gain_vec):
     grad_normed = grad_out * gain_vec
     mean_plain = jnp.mean(grad_normed, axis=1, keepdims=True)
     mean_mixed = jnp.mean(grad_normed * normed, axis=1, keepdims=True)
@@ -66,7 +1108,7 @@
     return (grad_in, jnp.sum(grad_out * normed, axis=0), jnp.sum(grad_out, axis=0))
 
 
-def shards(
+def plain_shards(
     tokens,
     teacher,
     lengths,
@@ -187,7 +1229,7 @@
         tiled=True,
     ).astype(jnp.float32)
     first_sum = tokens.astype(jnp.float32) + attn_out + small_wide[2]
-    hidden_one, normed_one, inv_one = norm_forward(first_sum, small_wide[3], small_wide[4])
+    hidden_one, normed_one, inv_one = plain_norm_forward(first_sum, small_wide[3], small_wide[4])
     hidden_low = hidden_one.astype(jnp.bfloat16)
     ffn_rows = ffn_gather(hidden_low)
     pre_act = plain_dot(ffn_rows, inner_full) + inner_mine
@@ -200,7 +1242,7 @@
         tiled=True,
     ).astype(jnp.float32)
     second_sum = hidden_one + ffn_out + small_wide[5]
-    final_rows, normed_two, inv_two = norm_forward(second_sum, small_wide[6], small_wide[7])
+    final_rows, normed_two, inv_two = plain_norm_forward(second_sum, small_wide[6], small_wide[7])
     layer_output = final_rows.astype(jnp.bfloat16)
     diff_rows = final_rows - teacher.astype(jnp.float32)
     loss_local = jnp.sum(counted * jnp.sum(diff_rows * diff_rows, axis=1))
@@ -218,7 +1260,7 @@
         innerb_full,
     ) = fetch_params()
     ffn_rows = ffn_gather(hidden_low)
-    grad_second, secondgain_part, secondshift_part = norm_backward(
+    grad_second, secondgain_part, secondshift_part = plain_norm_backward(
         grad_final, normed_two, inv_two, small_wide[6]
     )
     outerbias_part = jnp.sum(grad_second, axis=0)
@@ -238,7 +1280,7 @@
         lax.psum_scatter(inner_local, "dp", scatter_dimension=0, tiled=True),
         lax.psum_scatter(outer_local, "dp", scatter_dimension=1, tiled=True),
     )
-    grad_first, firstgain_part, firstshift_part = norm_backward(
+    grad_first, firstgain_part, firstshift_part = plain_norm_backward(
         grad_second + grad_hidden, normed_one, inv_one, small_wide[3]
     )
     mixerbias_part = jnp.sum(grad_first, axis=0)

time: 860 us -> 338 us (0.39)
  waiting for transfers between devices: 395 us -> 0 us
  Pallas kernels: 0 us -> 306 us
  matrix products: 188 us -> 0 us
  blocking collectives: 144 us -> 0 us
  other arithmetic: 68.8 us -> 6.05 us
  between operations: 20.5 us -> 4.55 us
  local copies, waits for them, and re-layouts: 29.3 us -> 19.8 us
  starting transfers between devices: 9.25 us -> 0 us
    pallas_call x0 -> x3, Pallas kernels: none -> 306 us  [the longest x1 140 us: front(): pl.pallas_call(front_kernel, name='front', out_shape=(S((4, rows, 192), B...]
    all_gather x6 -> x0, waiting for transfers between devices: 200 us -> none  [the longest x1 63.2 us: shards(): lax.all_gather(grad_first.astype(jnp.bfloat16), 'tensor', axis=0, tiled=T...]
    reduce_scatter x6 -> x0, waiting for transfers between devices: 193 us -> none  [the longest x1 59.1 us: shards(): lax.psum_scatter(contract_last(grad_pre, inner_full).astype(jnp.bfloat16)...]
    dot_general x46 -> x0, matrix products: 188 us -> none  [the longest x6 35.7 us: plain_dot(): return jnp.dot(left_rows, right_rows, preferred_element_type=jnp.float32)]
    psum x2 -> x0, blocking collectives: 87.7 us -> none  [shards(): lax.psum((loss_local, count_local), ('dp', 'tensor'))]
    all_gather x6 -> x0, blocking collectives: 56.2 us -> none  [the longest x1 10.4 us: fetch_params(): lax.all_gather(small_stack, 'dp', axis=1, tiled=True)]
    reduce_sum x17 -> x1, other arithmetic: 30.4 us -> 1.29 us  [shards(): jnp.sum(counted)]
    convert_element_type x9 -> x0, other arithmetic: 26 us -> none  [the longest x4 19.9 us: backward_block(): grad_scores = (prob_full * (grad_prob - row_dot)).astype(jnp.bfloat16)]
  transfers between devices with their start and end apart: 14 -> 0, of which waited for: 10 -> 0; matrix products, arithmetic and copies ran while one was open for 8% -> 0% of each run, Pallas kernels for 0% -> 0%
where the time goes in v1:
time: 338 us; the launch traced here: 337 us
  Pallas kernels  306 us (91%)
  local copies, waits for them, and re-layouts  19.8 us (6%)
  other arithmetic  6.05 us (2%)
  between operations  4.55 us (1%)
    pallas_call x1, Pallas kernels, front(): pl.pallas_call(front_kernel, name='front', out_shape=(S((4, rows, 192), B...  140 us
    pallas_call x1, Pallas kernels, back(): pl.pallas_call(back_kernel, name='back', out_shape=(S((rows, width), F32)...  132 us
    pallas_call x1, Pallas kernels, mid(): pl.pallas_call(mid_kernel, name='mid', out_shape=(S((rows, width), BF16),...  33.7 us

profile of v1, /device:TPU:0, one launch (start us, length us, event | category | flops | bytes accessed | tf_op | source)
XLA Modules:
  0.0 336.6 jit_solution(17818206750154762015)
XLA Ops:
  1.3 1.3 fusion.2
  2.6 0.6 broadcast_in_dim.22
  3.3 0.8 stack.35
  4.1 0.7 bitcast_convert_fusion
  4.8 1.2 concatenate.14.sm_ref
  6.0 0.9 copy.41
  6.8 1.7 pad_maximum_fusion.wm_ref
  8.6 1.6 pad_maximum_fusion.1.wq_ref
  10.2 140.0 %front.1 = (bf16[4,512,192]{2,1,0:T(8,128)(2,1)}, bf16[4,8,96,1728]{3,2,1,0:T(8,128)(2,1)}, f32[8,16,128]{2,1,0:T(8,128)}, f32[8,128]{1,0:T(8,128)}, bf16[4,512,...) custom-call(bf16[512,768]{1,0:T(8,128)(2,1)} %x_ref.3, ...), custom_call_target="tpu_custom_call" | custom-call | tf_op jit(solution)/shard_map/front/pallas_call | solution.py:444
  150.2 0.8 slice_bitcast_fusion.2
  151.0 0.7 reshape.71.vec_ref
  151.7 0.8 slice.65
  152.4 0.6 reshape_reshape.4.ib_ref
  153.1 1.2 slice.63
  155.6 0.9 copy.43.counted_ref
  156.5 33.7 %mid.1 = (bf16[512,768]{1,0:T(8,128)(2,1)}, f32[512,768]{1,0:T(8,128)}, bf16[4,512,192]{2,1,0:T(8,128)(2,1)}, bf16[4,768,1728]{2,1,0:T(8,128)(2,1)}, f32[8,768]{1,0:T(8,128)}, /*index=5*/f32[4,1,768]{2,1,0:T(1,128)}) custom-call(bf16[512,768]{1,0:T(8,128)(2,1)} %x_ref.3, bf16[512,768]{1,0:T(8,128)(2,1)} %teacher_ref.1, f32[512,1]{1,0:T(8,128)} %copy.43.counted_ref, ...), custom_call_target="tpu_custom_call" | custom-call | tf_op jit(solution)/shard_map/mid/pallas_call | solution.py:582
  190.2 0.8 reshape.73
  191.0 1.2 slice.67
  192.2 0.6 broadcast_in_dim.26
  192.9 0.7 reduce
  193.7 1.3 concatenate.15.pack_ref
  194.9 132.4 %back.1 = (f32[512,768]{1,0:T(8,128)}, f32[96,1728]{1,0:T(8,128)}, f32[96,576]{1,0:T(8,128)}, f32[16,128]{1,0:T(8,128)}) custom-call(bf16[4,512,192]{2,1,0:T(8,128)(2,1)} %get-tuple-element.44.do_ref, bf16[4,4,2,96,1728]{4,3,2,1,0:T(8,128)(2,1)} %bitcast.51, bf16[4,512,768]{2,1,0:T(8,128)(2,1)} %get-tuple-element.46.xs_ref, ...), custom_call_target="tpu_custom_call" | custom-call | tf_op jit(solution)/shard_map/back/pallas_call | solution.py:944
  327.4 0.0 copy-start.1
  327.4 0.0 copy-start
  327.4 2.0 fusion.4
  329.3 0.7 copy.46
  330.1 1.9 slice_bitcast_fusion
  332.0 0.0 copy-done.1
  332.0 0.5 slice_bitcast_fusion.4
  332.5 0.6 slice_bitcast_fusion.3
  333.1 0.5 slice.68
  334.3 0.0 copy-done
  334.3 1.1 copy.52
  (9 shorter events, 0.1 us)
Async XLA Ops:
  327.4 4.6 %copy-start.1 = (f32[16,128]{1,0:T(8,128)S(1)}, f32[16,128]{1,0:T(8,128)}, u32[]{:S(2)}) copy-start(f32[16,128]{1,0:T(8,128)} %get-tuple-element.56) | copy-start | bytes 24580
  327.4 6.9 %copy-start = (f32[512,768]{1,0:T(8,128)S(1)}, f32[512,768]{1,0:T(8,128)}, u32[]{:S(2)}) copy-start(f32[512,768]{1,0:T(8,128)} %get-tuple-element.132) | copy-start | bytes 4718596

commit v2 on v1

--- a/solution.py
+++ b/solution.py
@@ -55,6 +55,12 @@
         self.owner = self.base + self.pair
         self.near_here = 1 + self.pair
         self.near_there = 2 - self.pair
+        side = self.chip + 1 - 2 * lax.rem(self.chip, 2)
+        across = lax.rem(self.chip + 2, 4)
+        self.first = jnp.where(self.core == 0, side, across)
+        self.second = jnp.where(self.core == 0, across, side)
+        self.diagonal = 3 - self.chip
+        self.around = (self.buddy, self.near_there, 3 * (1 - self.pair))
 
 
 def greet(place):
@@ -127,6 +133,22 @@
         def _(s=s, dst=dst, target=target):
             remote(wq_ref, dst, wz_send.at[s], wz_recv.at[me.low], me.d, target).start()
 
+    is_near = me.z == me.near_here
+    is_end = jnp.logical_not(is_near)
+    pltpu.make_async_copy(wm_ref, wall_ref.at[me.z, me.d], mz_recv.at[me.z]).start()
+
+    def along_z(unit, t, sem, to):
+        return remote(unit, wall_ref.at[t, me.d], mz_send.at[sem], mz_recv.at[t], me.d, to)
+
+    pl.when(me.z > 0)(lambda: along_z(wm_ref, me.z, 0, me.z - 1).start())
+    pl.when(me.z < tp - 1)(lambda: along_z(wm_ref, me.z, 1, me.z + 1).start())
+
+    def goes_up(t):
+        return jnp.logical_and(t < me.z, me.z < tp - 1)
+
+    def goes_down(t):
+        return jnp.logical_and(t > me.z, me.z > 0)
+
     is_owner = me.core == me.pair
     for h in range(2):
         part = pl.ds(h * half, half)
@@ -141,11 +163,6 @@
         def _(h=h, part=part):
             remote(x_ref.at[part], xs_ref.at[me.z, part], x_send.at[h], x_recv.at[me.z, h], me.base + h, me.near_there).start()
 
-    pltpu.make_async_copy(wm_ref, wall_ref.at[me.z, me.d], mz_recv.at[me.z]).start()
-    for s in range(1, tp):
-        t = lax.rem(me.z + s, tp)
-        remote(wm_ref, wall_ref.at[me.z, me.d], mz_send.at[s - 1], mz_recv.at[me.z], me.d, t).start()
-
     def wq_plane(s, k):
         dst = wqf_ref.at[me.d]
         return remote(wqz.at[s], dst, wp_send.at[s, k], wp_recv.at[me.d], 2 * k + s, me.z)
@@ -169,18 +186,64 @@
 
         lax.fori_loop(0, chips, step, 0)
 
-    def plane_units(t):
-        def step(i, _):
-            k = lax.rem(me.chip + 1 + i, chips)
-            remote(
-                wall_ref.at[t, me.d], wall_ref.at[t, me.d], mp_send.at[t, i], mp_recv.at[t, me.chip], 2 * k + me.core, me.z
-            ).start()
-            return 0
-
-        lax.fori_loop(0, chips - 1, step, 0)
-
-    arrival(wall_ref.at[me.z, me.d], mz_recv.at[me.z]).wait()
-    plane_units(me.z)
+    def in_plane(unit, t, k, sem, to):
+        return remote(unit, wall_ref.at[t, 2 * k + me.core], mp_send.at[t, sem], mp_recv.at[t, k], 2 * to + me.core, me.z)
+
+    def plane_units(t, unit):
+        in_plane(unit, t, me.chip, 0, me.first).start()
+        in_plane(unit, t, me.chip, 1, me.second).start()
+
+    def to_sibling(t, k):
+        unit = wall_ref.at[t, 2 * k + me.core]
+        return remote(unit, unit, ms_send.at[t, k], ms_recv.at[t, k], me.sibling, me.z)
+
+    def own_unit(t):
+        unit = wall_ref.at[t, me.d]
+        arrival(unit, mz_recv.at[t]).wait()
+        pl.when(goes_up(t))(lambda: along_z(unit, t, 2 + t, me.z + 1).start())
+        pl.when(goes_down(t))(lambda: along_z(unit, t, 2 + t, me.z - 1).start())
+        plane_units(t, unit)
+        to_sibling(t, me.chip).start()
+
+    def plane_unit(t, k):
+        unit = wall_ref.at[t, 2 * k + me.core]
+        arrival(unit, mp_recv.at[t, k]).wait()
+        return unit
+
+    def plane_forward(t):
+        unit = plane_unit(t, me.first)
+        in_plane(unit, t, me.first, 2, me.second).start()
+        to_sibling(t, me.first).start()
+
+    def plane_rest(t):
+        for k in (me.second, me.diagonal):
+            plane_unit(t, k)
+            to_sibling(t, k).start()
+
+    plane_units(me.z, wm_ref)
+    remote(wm_ref, wall_ref.at[me.z, me.d], ms_send.at[me.z, me.chip], ms_recv.at[me.z, me.chip], me.sibling, me.z).start()
+
+    mine = pl.ds(pl.multiple_of(me.core * half, half), half)
+    other = pl.ds(pl.multiple_of((1 - me.core) * half, half), half)
+    far_first = 2 * (1 - me.pair) + me.pair
+    far_second = 2 * (1 - me.pair) + 1 - me.pair
+    blocks_in = (
+        jnp.where(is_near, far_first, me.buddy),
+        jnp.where(is_near, far_second, far_first),
+        jnp.where(is_near, me.buddy, far_second),
+    )
+
+    def relay(n):
+        j = blocks_in[n]
+        part = xs_ref.at[j, mine]
+        arrival(part, x_recv.at[j, me.core]).wait()
+        remote(part, part, xr_send.at[1 + n, 0], x_recv.at[j, me.core], me.sibling, me.z).start()
+        if n < 2:
+            pl.when(is_near)(lambda: remote(part, part, xf_send.at[n], x_recv.at[j, me.core], me.d, me.buddy).start())
+
+    own_unit(me.around[0])
+    relay(0)
+    relay(1)
 
     def small_wait(i, peer):
         arrival(smalls_ref.at[peer], sm_recv.at[peer]).wait()
@@ -254,37 +317,17 @@
             qT_ref[h, :, at] = jnp.where(srow == HEAD_DIM, BF16(1), qh)
             v_ref[h, at, :] = vals[:, span].astype(BF16)
 
-    def wait_half(j, h):
-        arrival(xs_ref.at[j, pl.ds(h * half, half)], x_recv.at[j, h]).wait()
-
-    mine = pl.ds(pl.multiple_of(me.core * half, half), half)
-
-    def relay(j, slot):
-        arrival(xs_ref.at[j, mine], x_recv.at[j, me.core]).wait()
-        remote(xs_ref.at[j, mine], xs_ref.at[j, mine], xr_send.at[slot, 0], x_recv.at[j, me.core], me.sibling, me.z).start()
-
-    wait_half(me.z, 0)
-    wait_half(me.z, 1)
+    arrival(xs_ref.at[me.z, pl.ds(0, half)], x_recv.at[me.z, 0]).wait()
+    arrival(xs_ref.at[me.z, pl.ds(half, half)], x_recv.at[me.z, 1]).wait()
     project(me.z)
-    relay(me.buddy, 1)
-    wait_half(me.buddy, 0) if False else None
-    far_first = 2 * (1 - me.pair) + me.pair
-    far_second = 2 * (1 - me.pair) + 1 - me.pair
-
-    is_near = me.z == me.near_here
-    for n, j in enumerate((far_first, far_second)):
-        relay(j, 2 + n)
-
-        @pl.when(is_near)
-        def _(n=n, j=j):
-            remote(xs_ref.at[j, mine], xs_ref.at[j, mine], xf_send.at[n], x_recv.at[j, me.core], me.d, me.buddy).start()
-
-        if n == 0:
-            arrival(xs_ref.at[me.buddy, pl.ds(pl.multiple_of((1 - me.core) * half, half), half)], x_recv.at[me.buddy, 1 - me.core]).wait()
-            project(me.buddy)
-    for j in (far_first, far_second):
-        arrival(xs_ref.at[j, pl.ds(pl.multiple_of((1 - me.core) * half, half), half)], x_recv.at[j, 1 - me.core]).wait()
+    relay(2)
+    pl.when(is_near)(functools.partial(own_unit, me.around[1]))
+    plane_forward(me.z)
+    for j in blocks_in:
+        arrival(xs_ref.at[j, other], x_recv.at[j, 1 - me.core]).wait()
         project(j)
+    pl.when(is_near)(functools.partial(own_unit, me.around[2]))
+    plane_forward(me.around[0])
 
     chunk = 256
     pieces = length // chunk
@@ -326,37 +369,21 @@
         def _():
             remote(o_buf.at[j], oin_ref.at[me.group], o_send.at[i], o_recv.at[me.group], me.owner, j).start()
 
-        @pl.when(i == 0)
-        def _():
-            for s in range(1, tp):
-                t = lax.rem(me.z + s, tp)
-                arrival(wall_ref.at[t, me.d], mz_recv.at[t]).wait()
-                plane_units(t)
-
+        for n in (1, 2):
+            pl.when(jnp.logical_and(is_end, i == n - 1))(functools.partial(own_unit, me.around[n]))
+        pl.when(i == 0)(functools.partial(plane_rest, me.z))
+        pl.when(jnp.logical_and(is_near, i == 0))(functools.partial(plane_forward, me.around[1]))
+        pl.when(jnp.logical_and(is_end, i == 2))(functools.partial(plane_forward, me.around[1]))
+        pl.when(jnp.logical_and(is_near, i == 2))(functools.partial(plane_forward, me.around[2]))
+        pl.when(jnp.logical_and(is_end, i == 3))(functools.partial(plane_forward, me.around[2]))
         return 0
 
     lax.fori_loop(0, tp, attend, 0)
 
-    def to_sibling(t, k):
-        unit = wall_ref.at[t, 2 * k + me.core]
-        return remote(unit, unit, ms_send.at[t, k], ms_recv.at[t, k], me.sibling, me.z)
-
-    def own_units(t, _):
-        to_sibling(t, me.chip).start()
-        return 0
-
-    lax.fori_loop(0, tp, own_units, 0)
-
-    def others(n, _):
-        i, s = n // tp, lax.rem(n, tp)
-        k = lax.rem(me.chip + 1 + i, chips)
-        t = lax.rem(me.z + s, tp)
-        arrival(wall_ref.at[t, 2 * k + me.core], mp_recv.at[t, k]).wait()
-        to_sibling(t, k).start()
-        return 0
-
-    lax.fori_loop(0, (chips - 1) * tp, others, 0)
-
+    for t in me.around:
+        plane_rest(t)
+
+    arrival(wall_ref.at[me.z, me.d], mz_recv.at[me.z]).wait()
     for s in range(1, tp):
         t = lax.rem(me.z + s, tp)
         arrival(counts.at[t], cn_recv.at[t]).wait()
@@ -377,7 +404,7 @@
 
     def sent(n, _):
         t, i = n // (chips - 1), lax.rem(n, chips - 1)
-        remote(wall_ref.at[t, me.d], wall_ref.at[t, me.d], mp_send.at[t, i], mp_recv.at[t, 0], me.sibling, me.z).wait_send()
+        in_plane(wm_ref, t, me.chip, i, me.first).wait_send()
         return 0
 
     lax.fori_loop(0, tp * (chips - 1), sent, 0)
@@ -400,7 +427,14 @@
         lax.fori_loop(0, chips, step, 0)
     for s in range(tp - 1):
         remote(counts.at[0], counts.at[0], cn_send.at[s], cn_recv.at[0], me.sibling, me.z).wait_send()
-        remote(wm_ref, wall_ref.at[0, 0], mz_send.at[s], mz_recv.at[0], me.sibling, me.z).wait_send()
+
+    def z_sent(sem):
+        along_z(wm_ref, 0, sem, 0).wait_send()
+
+    pl.when(me.z > 0)(functools.partial(z_sent, 0))
+    pl.when(me.z < tp - 1)(functools.partial(z_sent, 1))
+    for t in range(tp):
+        pl.when(jnp.logical_or(goes_up(t), goes_down(t)))(functools.partial(z_sent, 2 + t))
 
     def x_sent(sem):
         remote(x_ref.at[pl.ds(0, half)], xs_ref.at[0, pl.ds(0, half)], sem, x_recv.at[0, 0], me.sibling, me.z).wait_send()
@@ -457,7 +491,7 @@
             S((3, length, 128), BF16),
             S((3, length, 128), BF16),
         ),
-        in_specs=[vmem, vmem, anym, vmem],
+        in_specs=[vmem] * 4,
         out_specs=(anym, anym) + (vmem,) * 9,
         scratch_shapes=[
             pltpu.VMEM((2, share, wq.shape[1]), BF16),
@@ -472,7 +506,7 @@
             dma((dp - 1,)), dma((dp,)), dma((tp - 1,)), dma((tp,)),
             dma((2,)), dma((2,)), dma((2, chips)), dma((dp,)),
             dma((2,)), dma((tp, 2)), dma((4, 2)), dma((2,)),
-            dma((tp - 1,)), dma((tp,)), dma((tp, chips - 1)), dma((tp, chips)), dma((tp, chips)), dma((tp, chips)),
+            dma((tp + 2,)), dma((tp,)), dma((tp, chips - 1)), dma((tp, chips)), dma((tp, chips)), dma((tp, chips)),
             dma((tp,)), dma((4,)),
         ],
         compiler_params=pltpu.CompilerParams(
@@ -978,7 +1012,7 @@
     first_gain, first_shift, inner_weight, inner_bias, outer_weight, outer_bias, second_gain, second_shift,
 ):
     dp, tp = lax.axis_size("dp"), lax.axis_size("tensor")
-    if query_weight.shape[0] % 16 or tp != 4:
+    if dp != 8 or tp != 4:
         return plain_shards(
             tokens, teacher, lengths, loss_mask, loss_scale,
             query_weight, query_bias, key_weight, value_weight, value_bias, mixer_weight, mixer_bias,

time: 338 us -> 305 us (0.902)
  Pallas kernels: 306 us -> 273 us
    pallas_call x1, Pallas kernels: 140 us -> 107 us  [front(): pl.pallas_call(front_kernel, name='front', out_shape=(S((4, rows, 192), B...]
where the time goes in v2:
time: 305 us; the launch traced here: 303 us
  Pallas kernels  273 us (90%)
  local copies, waits for them, and re-layouts  19.8 us (6%)
  other arithmetic  6.05 us (2%)
  between operations  4.55 us (1%)
    pallas_call x1, Pallas kernels, back(): pl.pallas_call(back_kernel, name='back', out_shape=(S((rows, width), F32)...  132 us
    pallas_call x1, Pallas kernels, front(): pl.pallas_call(front_kernel, name='front', out_shape=(S((4, rows, 192), B...  107 us
    pallas_call x1, Pallas kernels, mid(): pl.pallas_call(mid_kernel, name='mid', out_shape=(S((rows, width), BF16),...  33.7 us

profile of v2, /device:TPU:0, one launch (start us, length us, event | category | flops | bytes accessed | tf_op | source)
XLA Modules:
  0.0 303.3 jit_solution(6868760955516740340)
XLA Ops:
  1.3 1.3 fusion.2
  2.6 0.6 broadcast_in_dim.22
  3.3 0.8 stack.35
  4.1 0.7 bitcast_convert_fusion
  4.8 1.2 concatenate.14.sm_ref
  6.0 0.9 copy.41
  6.8 1.7 pad_maximum_fusion.wm_ref
  8.6 1.6 pad_maximum_fusion.1.wq_ref
  10.2 106.8 %front.1 = (bf16[4,512,192]{2,1,0:T(8,128)(2,1)}, bf16[4,8,96,1728]{3,2,1,0:T(8,128)(2,1)}, f32[8,16,128]{2,1,0:T(8,128)}, f32[8,128]{1,0:T(8,128)}, bf16[4,512,...) custom-call(bf16[512,768]{1,0:T(8,128)(2,1)} %x_ref.3, ...), custom_call_target="tpu_custom_call" | custom-call | tf_op jit(solution)/shard_map/front/pallas_call | solution.py:478
  116.9 0.8 slice_bitcast_fusion.2
  117.7 0.7 reshape.71.vec_ref
  118.4 0.8 slice.65
  119.2 0.6 reshape_reshape.4.ib_ref
  119.8 1.2 slice.63
  122.3 0.9 copy.43.counted_ref
  123.2 33.7 %mid.1 = (bf16[512,768]{1,0:T(8,128)(2,1)}, f32[512,768]{1,0:T(8,128)}, bf16[4,512,192]{2,1,0:T(8,128)(2,1)}, bf16[4,768,1728]{2,1,0:T(8,128)(2,1)}, f32[8,768]{1,0:T(8,128)}, /*index=5*/f32[4,1,768]{2,1,0:T(1,128)}) custom-call(bf16[512,768]{1,0:T(8,128)(2,1)} %x_ref.3, bf16[512,768]{1,0:T(8,128)(2,1)} %teacher_ref.1, f32[512,1]{1,0:T(8,128)} %copy.43.counted_ref, ...), custom_call_target="tpu_custom_call" | custom-call | tf_op jit(solution)/shard_map/mid/pallas_call | solution.py:616
  156.9 0.8 reshape.73
  157.7 1.2 slice.67
  158.9 0.6 broadcast_in_dim.26
  159.6 0.7 reduce
  160.4 1.3 concatenate.15.pack_ref
  161.7 132.4 %back.1 = (f32[512,768]{1,0:T(8,128)}, f32[96,1728]{1,0:T(8,128)}, f32[96,576]{1,0:T(8,128)}, f32[16,128]{1,0:T(8,128)}) custom-call(bf16[4,512,192]{2,1,0:T(8,128)(2,1)} %get-tuple-element.44.do_ref, bf16[4,4,2,96,1728]{4,3,2,1,0:T(8,128)(2,1)} %bitcast.51, bf16[4,512,768]{2,1,0:T(8,128)(2,1)} %get-tuple-element.46.xs_ref, ...), custom_call_target="tpu_custom_call" | custom-call | tf_op jit(solution)/shard_map/back/pallas_call | solution.py:978
  294.1 0.0 copy-start.1
  294.1 0.0 copy-start
  294.1 2.0 fusion.4
  296.1 0.7 copy.46
  296.8 1.9 slice_bitcast_fusion
  298.7 0.0 copy-done.1
  298.7 0.5 slice_bitcast_fusion.4
  299.2 0.6 slice_bitcast_fusion.3
  299.8 0.5 slice.68
  301.0 0.0 copy-done
  301.0 1.1 copy.52
  (9 shorter events, 0.1 us)
Async XLA Ops:
  294.1 4.6 %copy-start.1 = (f32[16,128]{1,0:T(8,128)S(1)}, f32[16,128]{1,0:T(8,128)}, u32[]{:S(2)}) copy-start(f32[16,128]{1,0:T(8,128)} %get-tuple-element.56) | copy-start | bytes 24580
  294.1 6.9 %copy-start = (f32[512,768]{1,0:T(8,128)S(1)}, f32[512,768]{1,0:T(8,128)}, u32[]{:S(2)}) copy-start(f32[512,768]{1,0:T(8,128)} %get-tuple-element.132) | copy-start | bytes 4718596
